TPU v7x, 512 devices: a whole 4x8x8 slice. The times are simulated.
512 devices in a mesh: dp: 8 (over y_lo, core), ctx: 64 (over x, y_hi, z).
Axes of the slice: x: 4, y: 8 (y_hi: 2, y_lo: 4; y = y_hi * 4 + y_lo), z: 8, core: 2. Of those that a mesh axis runs over, the one named last changes fastest.
Arguments:
- tokens: bfloat16 [8, 32768, 1024], P('dp', 'ctx'), may hold values from -6 to 6
- w_query: bfloat16 [1024, 1024], P('dp')
- w_key: bfloat16 [1024, 1024], P('dp')
- w_value: bfloat16 [1024, 1024], P('dp'), may hold values from -0.1875 to 0.1875
- w_output: bfloat16 [1024, 1024], P('dp'), may hold values from -0.1875 to 0.1875
- nbr_index: int32 [8, 256, 8], P('dp', 'ctx'), may hold values from 0 to 255, as said below
- nbr_count: int32 [8, 256], P('dp', 'ctx'), may hold values from 1 to 8, as said below
Outputs:
- update: bfloat16 [8, 32768, 1024], P('dp', 'ctx')
Inputs may be any that keep to these rules, and one draw needn't show every extreme that they name: `nbr_index`: in each row the first nbr_count slots name distinct blocks, slot 0 names the query block itself, and every slot names a block at most 8 blocks away from it; unused slots name blocks of that same range. In every draw some block is exactly 8 away from a query block that uses it. `nbr_count`: in every draw some query block uses all 8 slots.
All inputs are finite; a program needn't handle non-finite values.
Results may differ from a plain program's by a relative error of at most 0.0089.
Values may be sent and summed in bfloat16 or wider, within the bound.
No kernel may reach another device: no remote copies, remote signals or barrier semaphores. Data moves between devices by JAX's collectives and lax.ppermute only.
A program may use at most 128 MiB of HBM per device.

v0:
```python
import jax
import jax.numpy as jnp
from jax import lax
from jax.sharding import PartitionSpec as P

HEADS = 8
HD = 128
BLK = 128
MAXN = 8
REACH = 2


def from_behind(value, axis, steps):
    count = lax.axis_size(axis)
    leading, last = (max(0, -steps), min(count, count - steps))
    return lax.ppermute(value, axis, [(source, source + steps) for source in range(leading, last)])


def attend_block(query_blk, key_sel, value_sel, used):
    query_heads = query_blk.reshape(BLK, HEADS, HD)
    key_heads = key_sel.reshape(MAXN * BLK, HEADS, HD)
    value_heads = value_sel.reshape(MAXN * BLK, HEADS, HD)
    scores = jnp.einsum(
        "qhd,khd->hqk", query_heads, key_heads, preferred_element_type=jnp.float32
    ) * HD ** (-0.5)
    slot_used = jnp.arange(MAXN * BLK) // BLK < used
    scores = jnp.where(slot_used[None, None, :], scores, -1e30)
    peak = jnp.max(scores, axis=-1, keepdims=True)
    expo = jnp.exp(scores - peak) * slot_used[None, None, :].astype(jnp.float32)
    weights = (expo / jnp.sum(expo, axis=-1, keepdims=True)).astype(jnp.bfloat16)
    attended = jnp.einsum("hqk,khd->qhd", weights, value_heads, preferred_element_type=jnp.float32)
    return attended.reshape(BLK, HEADS * HD).astype(jnp.bfloat16)


def move_far(payload, offset):
    return from_behind((payload[0], payload[1]), "ctx", offset)


def collect_window(payload):
    lower = []
    upper = []
    for offset in list(range(REACH, 0, -1)) + list(range(-1, -REACH - 1, -1)):
        moved = move_far(payload, offset)
        if offset > 0:
            lower.append(moved)
        else:
            upper.append(moved)
    return (lower, upper)


def project_pair(rows_in, full_key, full_value):
    keys = jnp.dot(rows_in, full_key, preferred_element_type=jnp.float32).astype(jnp.bfloat16)
    values = jnp.dot(rows_in, full_value, preferred_element_type=jnp.float32).astype(jnp.bfloat16)
    return (keys, values)


def gather_window(keys, values):
    lower, upper = collect_window((keys, values))
    pieces = lower + [(keys, values)] + upper
    key_window = jnp.concatenate([item[0] for item in pieces], axis=0)
    value_window = jnp.concatenate([item[1] for item in pieces], axis=0)
    return (key_window, value_window)


def body(tokens, w_query, w_key, w_value, w_output, nbr_index, nbr_count):
    local_tok = tokens[0]
    blocks = local_tok.shape[0] // BLK
    rank = lax.axis_index("ctx")
    values_f = local_tok.astype(jnp.float32)
    normed = (
        values_f * lax.rsqrt(jnp.mean(values_f * values_f, axis=-1, keepdims=True) + 1e-05)
    ).astype(jnp.bfloat16)
    full_query, full_key, full_value, full_output = (
        lax.all_gather(w_query, "dp", axis=0, tiled=True),
        lax.all_gather(w_key, "dp", axis=0, tiled=True),
        lax.all_gather(w_value, "dp", axis=0, tiled=True),
        lax.all_gather(w_output, "dp", axis=0, tiled=True),
    )
    keys, values = project_pair(normed, full_key, full_value)
    key_window, value_window = gather_window(keys, values)
    queries = jnp.dot(normed, full_query, preferred_element_type=jnp.float32).astype(jnp.bfloat16)
    width = HEADS * HD
    key_blocks = key_window.reshape(-1, BLK, width)
    value_blocks = value_window.reshape(-1, BLK, width)
    first_block = rank * blocks - REACH * blocks
    local_index = nbr_index[0] - first_block
    query_blocks = queries.reshape(blocks, BLK, width)

    def per_block(items):
        query_blk, index_row, used = items
        key_sel = jnp.take(key_blocks, index_row, axis=0)
        value_sel = jnp.take(value_blocks, index_row, axis=0)
        return attend_block(query_blk, key_sel, value_sel, used)

    attended = lax.map(per_block, (query_blocks, local_index, nbr_count[0])).reshape(
        blocks * BLK, width
    )
    update = jnp.dot(attended, full_output, preferred_element_type=jnp.float32).astype(jnp.bfloat16)
    return update[None]


def solution(mesh):
    placed = (
        P("dp", "ctx", None),
        P("dp", None),
        P("dp", None),
        P("dp", None),
        P("dp", None),
        P("dp", "ctx", None),
        P("dp", "ctx"),
    )
    return jax.shard_map(
        body, mesh=mesh, in_specs=placed, out_specs=P("dp", "ctx", None), check_vma=False
    )
```

profile of v0, /device:TPU:59, one launch (start us, length us, event | category | flops | bytes accessed | tf_op | source)
XLA Modules:
  0.0 534.2 jit_solution(2425077717888437057)
XLA Ops:
  10.3 45.3 %all-gather.9.cloned.1.call-done = bf16[1024,1024]{1,0:T(8,128)(2,1)} async-done(((bf16[128,1024]{1,0:T(8,128)(2,1)}), bf16[1024,1024]{1,0:T(8,128)(2,1)}) %all-gather.9.cloned.1.call-update) | async-done | bytes 2097168 | tf_op jit(solution)/shard_map/all_gather | solution.py:75
  55.6 3.2 convolution_convert_fusion.1
  58.8 4.3 collective-permute-start.4
  63.2 3.3 collective-permute-start.5
  66.5 33.6 %all-gather.5.cloned.1.call-done = bf16[1024,1024]{1,0:T(8,128)(2,1)} async-done(((bf16[128,1024]{1,0:T(8,128)(2,1)}), bf16[1024,1024]{1,0:T(8,128)(2,1)}) %all-gather.5.cloned.1.call-update) | async-done | bytes 2097168 | tf_op jit(solution)/shard_map/all_gather | solution.py:76
  102.9 3.4 collective-permute-start
  106.4 3.3 collective-permute-start.1
  109.7 76.0 %collective-permute-start.6 = (bf16[512,1024]{1,0:T(8,128)(2,1)S(1)}, bf16[512,1024]{1,0:T(8,128)(2,1)}, u32[]{:S(2)}, u32[]{:S(2)}) collective-permute-start(bf16[512,1024]{1,0:T(8,128)(2,1)S(1)} %convolution_convert_fusion.1), channel_id=1, source_target_pairs={{1,0},{2,1},{3,2},{4,3},{5,4},{6,5},{7,6},{8,7},{9,8},{10,9},{11,1... | collective-permute-start | bytes 3145736 | tf_op jit(solution)/shard_map/ppermute | solution.py:16
  185.7 4.3 collective-permute-start.7
  190.0 59.2 %all-gather.7.cloned.1.call-done = bf16[1024,1024]{1,0:T(8,128)(2,1)} async-done(((bf16[128,1024]{1,0:T(8,128)(2,1)}), bf16[1024,1024]{1,0:T(8,128)(2,1)}) %all-gather.7.cloned.1.call-update) | async-done | bytes 2097168 | tf_op jit(solution)/shard_map/all_gather | solution.py:74
  249.1 3.9 convolution_convert_fusion.2
  253.0 62.1 %collective-permute-start.2 = (bf16[512,1024]{1,0:T(8,128)(2,1)S(1)}, bf16[512,1024]{1,0:T(8,128)(2,1)S(1)}, u32[]{:S(2)}, u32[]{:S(2)}) collective-permute-start(bf16[512,1024]{1,0:T(8,128)(2,1)S(1)} %convolution_convert_fusion.3), channel_id=1, source_target_pairs={{1,0},{2,1},{3,2},{4,3},{5,4},{6,5},{7,6},{8,7},{9,8},{10,9},{11,1... | collective-permute-start | bytes 3145736 | tf_op jit(solution)/shard_map/ppermute | solution.py:16
  325.0 97.5 %collective-permute-done.2 = bf16[512,1024]{1,0:T(8,128)(2,1)S(1)} collective-permute-done((bf16[512,1024]{1,0:T(8,128)(2,1)S(1)}, bf16[512,1024]{1,0:T(8,128)(2,1)S(1)}, u32[]{:S(2)}, u32[]{:S(2)}) %collective-permute-start.2) | collective-permute-done | bytes 1048608 | tf_op jit(solution)/shard_map/ppermute | solution.py:16
  422.6 21.2 %collective-permute-done.3 = bf16[512,1024]{1,0:T(8,128)(2,1)S(1)} collective-permute-done((bf16[512,1024]{1,0:T(8,128)(2,1)S(1)}, bf16[512,1024]{1,0:T(8,128)(2,1)S(1)}, u32[]{:S(2)}, u32[]{:S(2)}) %collective-permute-start.3) | collective-permute-done | bytes 1048608 | tf_op jit(solution)/shard_map/ppermute | solution.py:16
  446.2 77.2 %while.12 = (s32[]{:T(128)}, bf16[4,128,1024]{2,1,0:T(8,128)(2,1)}, s32[4,8]{1,0:T(4,128)S(1)}, bf16[20,128,1024]{2,1,0:T(8,128)(2,1)}, s32[4]{0:T(128)S(1)}, /*...) while((s32[]{:T(128)}, bf16[4,128,1024]{2,1,0:T(8,128)(2,1)}, ...), condition=%wide.region_4.6_spmd, body=%wide.region_1.5_spmd.sunk | while | flops 548548672 | bytes 57170744 | solution.py:95
  449.4 4.5 gather_fusion.1
  453.9 3.4 broadcast_select_fusion.3
  468.7 4.5 gather_fusion.1
  473.2 3.4 broadcast_select_fusion.3
  488.1 4.5 gather_fusion.1
  492.6 3.4 broadcast_select_fusion.3
  507.4 4.5 gather_fusion.1
  511.9 3.4 broadcast_select_fusion.3
  523.5 4.1 fusion.22
  (105 shorter events, 64.4 us)
Async XLA Ops:
  6.5 49.1 %all-gather.9.cloned.1.call-start = ((), (), s32[]{:S(2)}) async-start(), calls=%async_computation.2 | async-start | bytes 2359296 | tf_op jit(solution)/shard_map/all_gather | solution.py:75
  7.3 92.8 %all-gather.5.cloned.1.call-start = ((), (), s32[]{:S(2)}) async-start(), calls=%async_computation | async-start | bytes 2359296 | tf_op jit(solution)/shard_map/all_gather | solution.py:76
  8.0 241.1 %all-gather.7.cloned.1.call-start = ((), (), s32[]{:S(2)}) async-start(), calls=%async_computation.1 | async-start | bytes 2359296 | tf_op jit(solution)/shard_map/all_gather | solution.py:74
  8.7 514.8 %all-gather.11.cloned.1.call-start = ((), (), s32[]{:S(2)}) async-start(), calls=%async_computation.3 | async-start | bytes 2359296 | tf_op jit(solution)/shard_map/all_gather | solution.py:77
  10.3 89.7 %copy-start.3 = (bf16[1,512,1024]{2,1,0:T(8,128)(2,1)S(1)}, bf16[1,512,1024]{2,1,0:T(8,128)(2,1)}, u32[]{:S(2)}) copy-start(bf16[1,512,1024]{2,1,0:T(8,128)(2,1)} %param.11) | copy-start | bytes 3145732
  58.8 50.9 %copy-start.4 = (s32[1,4,8]{2,1,0:T(4,128)S(1)}, s32[1,4,8]{2,1,0:T(4,128)}, u32[]{:S(2)}) copy-start(s32[1,4,8]{2,1,0:T(4,128)} %param.16) | copy-start | bytes 388
  58.8 126.9 %collective-permute-start.4 = (bf16[512,1024]{1,0:T(8,128)(2,1)S(1)}, bf16[512,1024]{1,0:T(8,128)(2,1)}, u32[]{:S(2)}, u32[]{:S(2)}) collective-permute-start(bf16[512,1024]{1,0:T(8,128)(2,1)S(1)} %convolution_convert_fusion.1), channel_id=1, source_target_pairs={{0,2},{1,3},{2,4},{3,5},{4,6},{5,7},{6,8},{7,9},{8,10},{9,11},{10,... | collective-permute-start | bytes 3145736 | tf_op jit(solution)/shard_map/ppermute | solution.py:16
  63.2 189.8 %collective-permute-start.5 = (bf16[512,1024]{1,0:T(8,128)(2,1)S(1)}, bf16[512,1024]{1,0:T(8,128)(2,1)}, u32[]{:S(2)}, u32[]{:S(2)}) collective-permute-start(bf16[512,1024]{1,0:T(8,128)(2,1)S(1)} %convolution_convert_fusion.1), channel_id=1, source_target_pairs={{0,1},{1,2},{2,3},{3,4},{4,5},{5,6},{6,7},{7,8},{8,9},{9,10},{10,1... | collective-permute-start | bytes 3145736 | tf_op jit(solution)/shard_map/ppermute | solution.py:16
  102.9 213.5 %collective-permute-start = (bf16[512,1024]{1,0:T(8,128)(2,1)S(1)}, bf16[512,1024]{1,0:T(8,128)(2,1)}, u32[]{:S(2)}, u32[]{:S(2)}) collective-permute-start(bf16[512,1024]{1,0:T(8,128)(2,1)S(1)} %convolution_convert_fusion.3), channel_id=1, source_target_pairs={{0,2},{1,3},{2,4},{3,5},{4,6},{5,7},{6,8},{7,9},{8,10},{9,11},{10,... | collective-permute-start | bytes 3145736 | tf_op jit(solution)/shard_map/ppermute | solution.py:16
  106.4 214.6 %collective-permute-start.1 = (bf16[512,1024]{1,0:T(8,128)(2,1)S(1)}, bf16[512,1024]{1,0:T(8,128)(2,1)}, u32[]{:S(2)}, u32[]{:S(2)}) collective-permute-start(bf16[512,1024]{1,0:T(8,128)(2,1)S(1)} %convolution_convert_fusion.3), channel_id=1, source_target_pairs={{0,1},{1,2},{2,3},{3,4},{4,5},{5,6},{6,7},{7,8},{8,9},{9,10},{10,1... | collective-permute-start | bytes 3145736 | tf_op jit(solution)/shard_map/ppermute | solution.py:16
  109.7 212.7 %collective-permute-start.6 = (bf16[512,1024]{1,0:T(8,128)(2,1)S(1)}, bf16[512,1024]{1,0:T(8,128)(2,1)}, u32[]{:S(2)}, u32[]{:S(2)}) collective-permute-start(bf16[512,1024]{1,0:T(8,128)(2,1)S(1)} %convolution_convert_fusion.1), channel_id=1, source_target_pairs={{1,0},{2,1},{3,2},{4,3},{5,4},{6,5},{7,6},{8,7},{9,8},{10,9},{11,1... | collective-permute-start | bytes 3145736 | tf_op jit(solution)/shard_map/ppermute | solution.py:16
  185.7 138.0 %collective-permute-start.7 = (bf16[512,1024]{1,0:T(8,128)(2,1)S(1)}, bf16[512,1024]{1,0:T(8,128)(2,1)}, u32[]{:S(2)}, u32[]{:S(2)}) collective-permute-start(bf16[512,1024]{1,0:T(8,128)(2,1)S(1)} %convolution_convert_fusion.1), channel_id=1, source_target_pairs={{2,0},{3,1},{4,2},{5,3},{6,4},{7,5},{8,6},{9,7},{10,8},{11,9},{12,... | collective-permute-start | bytes 3145736 | tf_op jit(solution)/shard_map/ppermute | solution.py:16
  253.0 169.6 %collective-permute-start.2 = (bf16[512,1024]{1,0:T(8,128)(2,1)S(1)}, bf16[512,1024]{1,0:T(8,128)(2,1)S(1)}, u32[]{:S(2)}, u32[]{:S(2)}) collective-permute-start(bf16[512,1024]{1,0:T(8,128)(2,1)S(1)} %convolution_convert_fusion.3), channel_id=1, source_target_pairs={{1,0},{2,1},{3,2},{4,3},{5,4},{6,5},{7,6},{8,7},{9,8},{10,9},{11,1... | collective-permute-start | bytes 3145736 | tf_op jit(solution)/shard_map/ppermute | solution.py:16
  316.4 127.4 %collective-permute-start.3 = (bf16[512,1024]{1,0:T(8,128)(2,1)S(1)}, bf16[512,1024]{1,0:T(8,128)(2,1)S(1)}, u32[]{:S(2)}, u32[]{:S(2)}) collective-permute-start(bf16[512,1024]{1,0:T(8,128)(2,1)S(1)} %convolution_convert_fusion.3), channel_id=1, source_target_pairs={{2,0},{3,1},{4,2},{5,3},{6,4},{7,5},{8,6},{9,7},{10,8},{11,9},{12,... | collective-permute-start | bytes 3145736 | tf_op jit(solution)/shard_map/ppermute | solution.py:16
  325.0 118.9 %copy-start.1 = (bf16[2560,1024]{1,0:T(8,128)(2,1)}, bf16[2560,1024]{1,0:T(8,128)(2,1)S(1)}, u32[]{:S(2)}) copy-start(bf16[2560,1024]{1,0:T(8,128)(2,1)S(1)} %constant_dynamic-update-slice_fusion.6) | copy-start | bytes 15728644
  325.0 121.2 %copy-start.5 = (s32[1,4]{1,0:T(1,128)S(1)}, s32[1,4]{1,0:T(1,128)}, u32[]{:S(2)}) copy-start(s32[1,4]{1,0:T(1,128)} %param.17) | copy-start | bytes 52
  443.9 2.3 copy-start.2
  461.1 1.7 copy-start
  480.4 1.7 copy-start
  499.7 1.7 copy-start
  519.0 1.7 copy-start
Sparse Core Ops, SparseCore 0:
  9.4 46.1 all-gather.8
  57.7 42.3 all-gather.4
  102.1 146.9 all-gather.6
  251.1 170.1 all-gather.10
where the time goes:
time: 535 us; the launch traced here: 534 us
  waiting for transfers between devices  259 us (48%)
  starting transfers between devices  159 us (30%)
  local copies, waits for them, and re-layouts  56.4 us (11%)
  other arithmetic  24.2 us (5%)
  matrix products  22.3 us (4%)
  between operations  13.4 us (3%)
    ppermute x8, starting transfers between devices, from_behind(): lax.ppermute(value, axis, [(source, source + steps) for source in range(l...  159 us
    ppermute x8, waiting for transfers between devices, from_behind(): lax.ppermute(value, axis, [(source, source + steps) for source in range(l...  119 us
    all_gather x1, waiting for transfers between devices, body(): lax.all_gather(w_query, 'dp', axis=0, tiled=True)  59.2 us
    all_gather x1, waiting for transfers between devices, body(): lax.all_gather(w_key, 'dp', axis=0, tiled=True)  45.3 us
    all_gather x1, waiting for transfers between devices, body(): lax.all_gather(w_value, 'dp', axis=0, tiled=True)  33.6 us
    gather x4, local copies, waits for them, and re-layouts, per_block(): key_sel = jnp.take(key_blocks, index_row, axis=0)  18 us
    select_n x4, other arithmetic, per_block(): value_sel = jnp.take(value_blocks, index_row, axis=0)  13.4 us
    gather x4, local copies, waits for them, and re-layouts, per_block(): value_sel = jnp.take(value_blocks, index_row, axis=0)  12.7 us
  transfers between devices with their start and end apart: 12, of which 5 were waited for; matrix products, arithmetic and copies ran while one was open for 18% of the time, Pallas kernels for 0%

commit v1 on v0

v1 whole, which is shorter than its diff:
```python
import numpy as np
import jax
import jax.numpy as jnp
from jax import lax
from jax.experimental import pallas as pl
from jax.experimental.pallas import tpu as pltpu
from jax.sharding import PartitionSpec as P

D = 1024
HEADS = 8
HD = 128
BLK = 128
MAXN = 8
REACH = 2
ROWS = 512
NDP = 8
NCTX = 64
BF = jnp.bfloat16
F32 = jnp.float32
SCALE2 = float(HD ** (-0.5) * np.log2(np.e))
VMEM_LIMIT = 60 << 20
AXES = ("dp", "ctx")


def flat(x, y, z, core):
    return ((y % 4) * 2 + core) * NCTX + (x % 4) * 16 + ((y % 8) // 4) * 8 + z % 8


def coords(index):
    dp, ctx = divmod(index, NCTX)
    return ctx // 16, (ctx // 8 % 2) * 4 + dp // 2, ctx % 8, dp % 2


def routes(target):
    return [(i, flat(*target(*coords(i)))) for i in range(NDP * NCTX)]


def ctx_routes(step, keep=lambda r: True):
    return [
        (dp * NCTX + r, dp * NCTX + r + step)
        for dp in range(NDP)
        for r in range(NCTX)
        if 0 <= r + step < NCTX and keep(r)
    ]


FROM_UP = routes(lambda x, y, z, c: (x, y - 1, z, c))
FROM_DOWN = routes(lambda x, y, z, c: (x, y + 1, z, c))
FROM_FAR = routes(lambda x, y, z, c: (x, y + 2 if y % 2 == 0 else y - 2, z, c))
SHIFTS = (1, -1, 2)
X_NEXT = routes(lambda x, y, z, c: (x + 1, y, z, c))
X_PREV = routes(lambda x, y, z, c: (x - 1, y, z, c))
SIBLING = routes(lambda x, y, z, c: (x, y, z, 1 - c))


def send(value, pairs):
    return lax.ppermute(value, AXES, pairs)


def normalise(tok):
    v = tok.astype(F32)
    return (v * lax.rsqrt(jnp.mean(v * v, axis=-1, keepdims=True) + 1e-05)).astype(BF)


def piece_copies(pos, srcs, picks, dst, sem):
    ylo, core, par = pos[0], pos[1], pos[2]
    own, sib, mine, other, sib_mine, sib_other = srcs
    copies = []

    def add(src, row, n, col):
        copies.append(
            pltpu.make_async_copy(
                src, dst.at[pl.ds(pl.multiple_of(row, 64), n), pl.ds(col, D)], sem
            )
        )

    for at, w in enumerate(picks):
        add(own.at[w], (ylo * 2 + core) * 128, 128, at * D)
        add(sib.at[w], (ylo * 2 + 1 - core) * 128, 128, at * D)
        for i, s in enumerate(SHIFTS):
            base = lax.rem(ylo + s + 4, 4) * 2
            row = (base + core) * 128
            row_sib = (base + 1 - core) * 128
            add(mine.at[i, w], row + par * 64, 64, at * D)
            add(other.at[i, w % 2], row + (1 - par) * 64, 64, at * D)
            add(sib_mine.at[i, w], row_sib + par * 64, 64, at * D)
            add(sib_other.at[i, w % 2], row_sib + (1 - par) * 64, 64, at * D)
    return copies


def first_proj_kernel(pos, tok, *refs):
    srcs, (out, w_out, w_buf, sem, sem2) = refs[:6], refs[6:]
    copies = piece_copies(pos, srcs, (0, 1), w_buf, sem)
    for c in copies:
        c.start()
    for c in copies:
        c.wait()
    save = pltpu.make_async_copy(w_buf, w_out, sem2)
    save.start()
    for i in range(0, ROWS, 256):
        rows = slice(i, i + 256)
        out[rows, :] = jnp.dot(
            normalise(tok[rows, :]), w_buf[...], preferred_element_type=F32
        ).astype(BF)
    save.wait()


def proj_kernel(tok, w, out):
    out[...] = jnp.dot(normalise(tok[...]), w[...], preferred_element_type=F32).astype(BF)


def query_kernel(pos, tok, *refs):
    srcs, (out, w_out, w_buf, sem, sem2) = refs[:6], refs[6:]
    copies = piece_copies(pos, srcs, (2, 3), w_buf, sem)
    for c in copies:
        c.start()
    for c in copies:
        c.wait()
    save = pltpu.make_async_copy(w_buf.at[:, pl.ds(D, D)], w_out, sem2)
    save.start()
    out[...] = jnp.dot(
        normalise(tok[...]), w_buf[:, :D], preferred_element_type=F32
    ).astype(BF)
    save.wait()


def final_kernel(
    idx, cnt, low2, up2, query, w_kv, w_o, kv_low, kv_own, kv_up, out, kv, w_buf, wo_buf, att, sem
):
    get_w = pltpu.make_async_copy(w_kv, w_buf, sem.at[0])
    get_w.start()
    gets = [
        pltpu.make_async_copy(src, kv.at[pl.ds((i + 1) * ROWS, ROWS)], sem.at[1 + i])
        for i, src in enumerate((kv_low, kv_own, kv_up))
    ]
    gets.append(pltpu.make_async_copy(w_o, wo_buf, sem.at[4]))
    for g in gets:
        g.start()
    get_w.wait()
    for tok, base in ((low2, 0), (up2, 4 * ROWS)):
        for i in range(0, ROWS, 256):
            kv[base + i : base + i + 256, :] = jnp.dot(
                normalise(tok[i : i + 256, :]), w_buf[...], preferred_element_type=F32
            ).astype(BF)
    for g in gets:
        g.wait()

    def one_block(b, carry):
        used = cnt[b]
        rows = pl.ds(pl.multiple_of(b * BLK, BLK), BLK)
        starts = [pl.multiple_of(idx[b, j] * BLK, BLK) for j in range(MAXN)]
        for h in range(HEADS):
            hs = pl.ds(h * HD, HD)
            q = query[rows, hs]
            scores = []
            for j in range(MAXN):
                s = lax.dot_general(
                    q, kv[pl.ds(starts[j], BLK), hs], (((1,), (1,)), ((), ())),
                    preferred_element_type=F32,
                )
                scores.append(jnp.where(j < used, s, -1e30))
            peak = scores[0]
            for s in scores[1:]:
                peak = jnp.maximum(peak, s)
            peak = jnp.max(peak, axis=-1, keepdims=True)
            expo = [jnp.exp2((s - peak) * SCALE2) for s in scores]
            total = expo[0]
            for e in expo[1:]:
                total = total + e
            total = jnp.sum(total, axis=-1, keepdims=True)
            acc = jnp.zeros((BLK, HD), F32)
            for j in range(0, MAXN, 2):
                vals = jnp.concatenate(
                    [kv[pl.ds(starts[i], BLK), pl.ds(D + h * HD, HD)] for i in (j, j + 1)], axis=0
                )
                wts = jnp.concatenate([expo[j].astype(BF), expo[j + 1].astype(BF)], axis=1)
                acc = acc + jnp.dot(wts, vals, preferred_element_type=F32)
            att[rows, hs] = (acc / total).astype(BF)
        return carry

    lax.fori_loop(0, ROWS // BLK, one_block, 0)
    for i in range(0, ROWS, 256):
        out[i : i + 256, :] = jnp.dot(
            att[i : i + 256, :], wo_buf[...], preferred_element_type=F32
        ).astype(BF)


def body(tokens, w_query, w_key, w_value, w_output, nbr_index, nbr_count):
    tok = tokens[0]
    dp = lax.axis_index("dp")
    rank = lax.axis_index("ctx")
    ylo, core, par = dp // 2, dp % 2, (rank // 16) % 2
    pos = jnp.stack([ylo, core, par]).astype(jnp.int32)

    up, down = ctx_routes(1), ctx_routes(-1)
    own = jnp.stack([w_key, w_value, w_query, w_output])
    half = lax.dynamic_slice_in_dim(own, par * 64, 64, axis=1)
    mine = jnp.stack([send(half, p) for p in (FROM_UP, FROM_DOWN, FROM_FAR)])
    low = send(tok, up)
    high = send(tok, down)
    sib = send(own, SIBLING)
    other_kv = send(mine[:, :2], X_NEXT)
    other_qo = send(mine[:, 2:], X_PREV)
    sib_mine = send(mine, SIBLING)
    sib_kv = send(other_kv, SIBLING)
    sib_qo = send(other_qo, SIBLING)
    low2 = send(low, up)
    high2 = send(high, down)

    vm = pl.BlockSpec(memory_space=pltpu.VMEM)
    anyspace = pl.BlockSpec(memory_space=pl.ANY)
    smem = pl.BlockSpec(memory_space=pltpu.SMEM)
    params = pltpu.CompilerParams(vmem_limit_bytes=VMEM_LIMIT)
    pieces_kv = (own, sib, mine, other_kv, sib_mine, sib_kv)
    pieces_qo = (own, sib, mine, other_qo, sib_mine, sib_qo)
    kv_own, w_kv = pl.pallas_call(
        first_proj_kernel,
        in_specs=[smem, vm] + [anyspace] * 6,
        out_specs=[vm, anyspace],
        out_shape=[
            jax.ShapeDtypeStruct((ROWS, 2 * D), BF),
            jax.ShapeDtypeStruct((D, 2 * D), BF),
        ],
        scratch_shapes=[
            pltpu.VMEM((D, 2 * D), BF),
            pltpu.SemaphoreType.DMA,
            pltpu.SemaphoreType.DMA,
        ],
        compiler_params=params,
        name="first_proj",
    )(pos, tok, *pieces_kv)

    def project(t):
        return pl.pallas_call(
            proj_kernel,
            grid=(2,),
            in_specs=[
                pl.BlockSpec((256, D), lambda i: (i, 0)),
                pl.BlockSpec((D, 2 * D), lambda i: (0, 0), pipeline_mode=pl.Buffered(1)),
            ],
            out_specs=pl.BlockSpec((256, 2 * D), lambda i: (i, 0)),
            out_shape=jax.ShapeDtypeStruct((ROWS, 2 * D), BF),
            compiler_params=params,
            name="proj",
        )(t, w_kv)

    kv_low = project(low)
    kv_high = project(high)
    query, w_o = pl.pallas_call(
        query_kernel,
        in_specs=[smem, vm] + [anyspace] * 6,
        out_specs=[vm, anyspace],
        out_shape=[jax.ShapeDtypeStruct((ROWS, D), BF), jax.ShapeDtypeStruct((D, D), BF)],
        scratch_shapes=[
            pltpu.VMEM((D, 2 * D), BF),
            pltpu.SemaphoreType.DMA,
            pltpu.SemaphoreType.DMA,
        ],
        compiler_params=params,
        name="query",
    )(pos, tok, *pieces_qo)
    index = nbr_index[0] - (rank * (ROWS // BLK) - REACH * (ROWS // BLK))
    update = pl.pallas_call(
        final_kernel,
        in_specs=[smem, smem, vm, vm, vm] + [anyspace] * 5,
        out_specs=vm,
        out_shape=jax.ShapeDtypeStruct((ROWS, D), BF),
        scratch_shapes=[
            pltpu.VMEM((5 * ROWS, 2 * D), BF),
            pltpu.VMEM((D, 2 * D), BF),
            pltpu.VMEM((D, D), BF),
            pltpu.VMEM((ROWS, D), BF),
            pltpu.SemaphoreType.DMA((5,)),
        ],
        compiler_params=params,
        name="final",
    )(index, nbr_count[0], low2, high2, query, w_kv, w_o, kv_low, kv_own, kv_high)
    return update[None]


def solution(mesh):
    placed = (
        P("dp", "ctx", None),
        P("dp", None),
        P("dp", None),
        P("dp", None),
        P("dp", None),
        P("dp", "ctx", None),
        P("dp", "ctx"),
    )
    return jax.shard_map(
        body, mesh=mesh, in_specs=placed, out_specs=P("dp", "ctx", None), check_vma=False
    )
```

time: 535 us -> 173 us (0.32)
  the two profiles are of different devices: /device:TPU:59 before, /device:TPU:49 now
where the time goes in v1:
time: 173 us; the launch traced here: 172 us
  starting transfers between devices  76.8 us (44%)
  Pallas kernels  51.4 us (30%)
  waiting for transfers between devices  39.6 us (23%)
  other arithmetic  2.65 us (2%)
    ppermute x13, starting transfers between devices, send(): return lax.ppermute(value, AXES, pairs)  76.8 us
    ppermute x13, waiting for transfers between devices, send(): return lax.ppermute(value, AXES, pairs)  39.6 us
    pallas_call x1, Pallas kernels, body(): pl.pallas_call(final_kernel, in_specs=[smem, smem, vm, vm, vm] + [anyspac...  26 us
    pallas_call x2, Pallas kernels, project(): pl.pallas_call(proj_kernel, grid=(2,), in_specs=[pl.BlockSpec((256, D), l...  12.4 us
    pallas_call x1, Pallas kernels, body(): pl.pallas_call(first_proj_kernel, in_specs=[smem, vm] + [anyspace] * 6, o...  7.19 us
    pallas_call x1, Pallas kernels, body(): pl.pallas_call(query_kernel, in_specs=[smem, vm] + [anyspace] * 6, out_sp...  5.79 us
  transfers between devices with their start and end apart: 13, of which 2 were waited for; matrix products, arithmetic and copies ran while one was open for 1% of the time, Pallas kernels for 15%

profile of v1, /device:TPU:49, one launch (start us, length us, event | category | flops | bytes accessed | tf_op | source)
XLA Modules:
  0.0 172.1 jit_solution(10147378162783444213)
XLA Ops:
  0.0 1.3 pad_maximum_fusion.1.refs_0_
  1.3 2.6 %collective-permute-start.4 = (bf16[4,128,1024]{2,1,0:T(8,128)(2,1)S(1)}, bf16[4,128,1024]{2,1,0:T(8,128)(2,1)}, u32[]{:S(2)}, u32[]{:S(2)}) collective-permute-start(bf16[4,128,1024]{2,1,0:T(8,128)(2,1)S(1)} %pad_maximum_fusion.1.refs_0_), channel_id=1, source_target_pairs={{0,64},{1,65},{2,66},{3,67},{4,68},{5,69},{6,70},{7,71},{8,72},{9,... | collective-permute-start | bytes 3145736 | tf_op jit(solution)/shard_map/ppermute | solution.py:57
  4.0 6.9 %collective-permute-start.7 = (bf16[4,64,1024]{2,1,0:T(8,128)(2,1)S(1)}, bf16[4,64,1024]{2,1,0:T(8,128)(2,1)S(1)}, u32[]{:S(2)}, u32[]{:S(2)}) collective-permute-start(bf16[4,64,1024]{2,1,0:T(8,128)(2,1)S(1)} %constant_dynamic-slice_fusion), channel_id=1, source_target_pairs={{0,256},{1,257},{2,258},{3,259},{4,260},{5,261},{6,262},{7,263},{8... | collective-permute-start | bytes 1572872 | tf_op jit(solution)/shard_map/ppermute | solution.py:57
  10.9 1.9 %collective-permute-start.6 = (bf16[4,64,1024]{2,1,0:T(8,128)(2,1)S(1)}, bf16[4,64,1024]{2,1,0:T(8,128)(2,1)S(1)}, u32[]{:S(2)}, u32[]{:S(2)}) collective-permute-start(bf16[4,64,1024]{2,1,0:T(8,128)(2,1)S(1)} %constant_dynamic-slice_fusion), channel_id=1, source_target_pairs={{0,128},{1,129},{2,130},{3,131},{4,132},{5,133},{6,134},{7,135},{8... | collective-permute-start | bytes 1572872 | tf_op jit(solution)/shard_map/ppermute | solution.py:57
  12.8 3.4 %collective-permute-start.5 = (bf16[4,64,1024]{2,1,0:T(8,128)(2,1)S(1)}, bf16[4,64,1024]{2,1,0:T(8,128)(2,1)S(1)}, u32[]{:S(2)}, u32[]{:S(2)}) collective-permute-start(bf16[4,64,1024]{2,1,0:T(8,128)(2,1)S(1)} %constant_dynamic-slice_fusion), channel_id=1, source_target_pairs={{0,392},{1,393},{2,394},{3,395},{4,396},{5,397},{6,398},{7,399},{8... | collective-permute-start | bytes 1572872 | tf_op jit(solution)/shard_map/ppermute | solution.py:57
  16.2 10.6 %collective-permute-start.2 = (bf16[512,1024]{1,0:T(8,128)(2,1)}, bf16[512,1024]{1,0:T(8,128)(2,1)}, u32[]{:S(2)}, u32[]{:S(2)}) collective-permute-start(bf16[512,1024]{1,0:T(8,128)(2,1)} %bitcast.2.tok), channel_id=1, source_target_pairs={{1,0},{2,1},{3,2},{4,3},{5,4},{6,5},{7,6},{8,7},{9,8},{10,9},{11,1... | collective-permute-start | bytes 3145736 | tf_op jit(solution)/shard_map/ppermute | solution.py:57
  26.8 1.9 %collective-permute-start = (bf16[512,1024]{1,0:T(8,128)(2,1)}, bf16[512,1024]{1,0:T(8,128)(2,1)}, u32[]{:S(2)}, u32[]{:S(2)}) collective-permute-start(bf16[512,1024]{1,0:T(8,128)(2,1)} %bitcast.2.tok), channel_id=1, source_target_pairs={{0,1},{1,2},{2,3},{3,4},{4,5},{5,6},{6,7},{7,8},{8,9},{9,10},{10,1... | collective-permute-start | bytes 3145736 | tf_op jit(solution)/shard_map/ppermute | solution.py:57
  28.7 27.3 %collective-permute-done.6 = bf16[4,64,1024]{2,1,0:T(8,128)(2,1)S(1)} collective-permute-done((bf16[4,64,1024]{2,1,0:T(8,128)(2,1)S(1)}, bf16[4,64,1024]{2,1,0:T(8,128)(2,1)S(1)}, u32[]{:S(2)}, u32[]{:S(2)}) %collective-permute-start.6) | collective-permute-done | bytes 524320 | tf_op jit(solution)/shard_map/ppermute | solution.py:57
  56.3 1.9 %collective-permute-start.11 = (bf16[3,2,64,1024]{3,2,1,0:T(8,128)(2,1)S(1)}, bf16[3,2,64,1024]{3,2,1,0:T(8,128)(2,1)}, u32[]{:S(2)}, u32[]{:S(2)}) collective-permute-start(bf16[3,2,64,1024]{3,2,1,0:T(8,128)(2,1)S(1)} %get-tuple-element.13), channel_id=1, source_target_pairs={{0,16},{1,17},{2,18},{3,19},{4,20},{5,21},{6,22},{7,23},{8,24},{9,... | collective-permute-start | bytes 2359304 | tf_op jit(solution)/shard_map/ppermute | solution.py:57
  58.3 3.1 %collective-permute-start.9 = (bf16[3,4,64,1024]{3,2,1,0:T(8,128)(2,1)S(1)}, bf16[3,4,64,1024]{3,2,1,0:T(8,128)(2,1)}, u32[]{:S(2)}, u32[]{:S(2)}) collective-permute-start(bf16[3,4,64,1024]{3,2,1,0:T(8,128)(2,1)S(1)} %pad_maximum_fusion.refs_2_), channel_id=1, source_target_pairs={{0,64},{1,65},{2,66},{3,67},{4,68},{5,69},{6,70},{7,71},{8,72},{9,... | collective-permute-start | bytes 4718600 | tf_op jit(solution)/shard_map/ppermute | solution.py:57
  61.4 4.9 %collective-permute-start.8 = (bf16[3,2,64,1024]{3,2,1,0:T(8,128)(2,1)S(1)}, bf16[3,2,64,1024]{3,2,1,0:T(8,128)(2,1)S(1)}, u32[]{:S(2)}, u32[]{:S(2)}) collective-permute-start(bf16[3,2,64,1024]{3,2,1,0:T(8,128)(2,1)S(1)} %get-tuple-element.14), channel_id=1, source_target_pairs={{0,48},{1,49},{2,50},{3,51},{4,52},{5,53},{6,54},{7,55},{8,56},{9,... | collective-permute-start | bytes 2359304 | tf_op jit(solution)/shard_map/ppermute | solution.py:57
  66.3 12.3 %collective-permute-done.2.tok = bf16[512,1024]{1,0:T(8,128)(2,1)} collective-permute-done((bf16[512,1024]{1,0:T(8,128)(2,1)}, bf16[512,1024]{1,0:T(8,128)(2,1)}, u32[]{:S(2)}, u32[]{:S(2)}) %collective-permute-start.2) | collective-permute-done | bytes 1048608 | tf_op jit(solution)/shard_map/ppermute | solution.py:57
  78.6 10.1 %collective-permute-start.3 = (bf16[512,1024]{1,0:T(8,128)(2,1)}, bf16[512,1024]{1,0:T(8,128)(2,1)S(1)}, u32[]{:S(2)}, u32[]{:S(2)}) collective-permute-start(bf16[512,1024]{1,0:T(8,128)(2,1)} %collective-permute-done.2.tok), channel_id=1, source_target_pairs={{1,0},{2,1},{3,2},{4,3},{5,4},{6,5},{7,6},{8,7},{9,8},{10,9},{11,1... | collective-permute-start | bytes 3145736 | tf_op jit(solution)/shard_map/ppermute | solution.py:57
  88.7 1.9 %collective-permute-start.1 = (bf16[512,1024]{1,0:T(8,128)(2,1)}, bf16[512,1024]{1,0:T(8,128)(2,1)}, u32[]{:S(2)}, u32[]{:S(2)}) collective-permute-start(bf16[512,1024]{1,0:T(8,128)(2,1)} %collective-permute-done.tok), channel_id=1, source_target_pairs={{0,1},{1,2},{2,3},{3,4},{4,5},{5,6},{6,7},{7,8},{8,9},{9,10},{10,1... | collective-permute-start | bytes 3145736 | tf_op jit(solution)/shard_map/ppermute | solution.py:57
  90.6 25.7 %collective-permute-start.12 = (bf16[3,2,64,1024]{3,2,1,0:T(8,128)(2,1)}, bf16[3,2,64,1024]{3,2,1,0:T(8,128)(2,1)}, u32[]{:S(2)}, u32[]{:S(2)}) collective-permute-start(bf16[3,2,64,1024]{3,2,1,0:T(8,128)(2,1)} %collective-permute-done.11.refs_3_), channel_id=1, source_target_pairs={{0,64},{1,65},{2,66},{3,67},{4,68},{5,69},{6,70},{7,71},{8,72},{9,... | collective-permute-start | bytes 2359304 | tf_op jit(solution)/shard_map/ppermute | solution.py:57
  116.4 1.9 %collective-permute-start.10 = (bf16[3,2,64,1024]{3,2,1,0:T(8,128)(2,1)S(1)}, bf16[3,2,64,1024]{3,2,1,0:T(8,128)(2,1)}, u32[]{:S(2)}, u32[]{:S(2)}) collective-permute-start(bf16[3,2,64,1024]{3,2,1,0:T(8,128)(2,1)S(1)} %collective-permute-done.8.refs_3_), channel_id=1, source_target_pairs={{0,64},{1,65},{2,66},{3,67},{4,68},{5,69},{6,70},{7,71},{8,72},{9,... | collective-permute-start | bytes 2359304 | tf_op jit(solution)/shard_map/ppermute | solution.py:57
  118.3 0.6 pad_add_fusion.pos
  118.9 0.6 subtract_bitcast_fusion.idx
  119.5 7.2 %first_proj.1 = (bf16[512,2048]{1,0:T(8,128)(2,1)}, bf16[1024,2048]{1,0:T(8,128)(2,1)}) custom-call(s32[3]{0:T(128)} %pad_add_fusion.pos, bf16[512,1024]{1,0:T(8,128)(2,1)} %bitcast.2.tok, bf16[4,128,1024]{2,1,0:T(8,128)(2,1)} %copy-done.1, bf16[4,128,1024]{2,1,0:T(8,128)(2,1)} %collective-permute-done.4.refs_1_, bf16[3,4,64,1024]{3,2,1,0:T(8,128)(2,1)} %copy-done, ...), custom_call_target="tpu_custom_call" | custom-call | tf_op jit(solution)/shard_map/first_proj/pallas_call | solution.py:216
  126.7 6.3 %proj.3.kv_up = bf16[512,2048]{1,0:T(8,128)(2,1)} custom-call(bf16[512,1024]{1,0:T(8,128)(2,1)} %collective-permute-done.2.tok, bf16[1024,2048]{1,0:T(8,128)(2,1)} %get-tuple-element.10.w.w_kv), custom_call_target="tpu_custom_call" | custom-call | tf_op jit(solution)/shard_map/proj/pallas_call | solution.py:234
  133.0 6.1 %proj.2.kv_low = bf16[512,2048]{1,0:T(8,128)(2,1)} custom-call(bf16[512,1024]{1,0:T(8,128)(2,1)} %collective-permute-done.tok, bf16[1024,2048]{1,0:T(8,128)(2,1)} %get-tuple-element.10.w.w_kv), custom_call_target="tpu_custom_call" | custom-call | tf_op jit(solution)/shard_map/proj/pallas_call | solution.py:234
  139.1 5.8 %query.1 = (bf16[512,1024]{1,0:T(8,128)(2,1)}, bf16[1024,1024]{1,0:T(8,128)(2,1)}) custom-call(s32[3]{0:T(128)} %pad_add_fusion.pos, bf16[512,1024]{1,0:T(8,128)(2,1)} %bitcast.2.tok, bf16[4,128,1024]{2,1,0:T(8,128)(2,1)} %copy-done.1, bf16[4,128,1024]{2,1,0:T(8,128)(2,1)} %collective-permute-done.4.refs_1_, bf16[3,4,64,1024]{3,2,1,0:T(8,128)(2,1)} %copy-done, ...), custom_call_target="tpu_custom_call" | custom-call | tf_op jit(solution)/shard_map/query/pallas_call | solution.py:249
  144.9 1.0 copy-done.2
  145.9 26.0 %final.1 = bf16[512,1024]{1,0:T(8,128)(2,1)} custom-call(s32[4,8]{1,0:T(4,128)} %subtract_bitcast_fusion.idx, s32[4]{0:T(128)} %bitcast.22, bf16[512,1024]{1,0:T(8,128)(2,1)} %collective-permute-done.1.low2, bf16[512,1024]{1,0:T(8,128)(2,1)} %copy-done.2, bf16[512,1024]{1,0:T(8,128)(2,1)} %get-tuple-element.9.query, ...), custom_call_target="tpu_custom_call" | custom-call | tf_op jit(solution)/shard_map/final/pallas_call | solution.py:263
  (23 shorter events, 0.4 us)
Async XLA Ops:
  1.3 54.8 %copy-start.1 = (bf16[4,128,1024]{2,1,0:T(8,128)(2,1)}, bf16[4,128,1024]{2,1,0:T(8,128)(2,1)S(1)}, u32[]{:S(2)}) copy-start(bf16[4,128,1024]{2,1,0:T(8,128)(2,1)S(1)} %pad_maximum_fusion.1.refs_0_) | copy-start | bytes 3145732
  1.3 60.1 %collective-permute-start.4 = (bf16[4,128,1024]{2,1,0:T(8,128)(2,1)S(1)}, bf16[4,128,1024]{2,1,0:T(8,128)(2,1)}, u32[]{:S(2)}, u32[]{:S(2)}) collective-permute-start(bf16[4,128,1024]{2,1,0:T(8,128)(2,1)S(1)} %pad_maximum_fusion.1.refs_0_), channel_id=1, source_target_pairs={{0,64},{1,65},{2,66},{3,67},{4,68},{5,69},{6,70},{7,71},{8,72},{9,... | collective-permute-start | bytes 3145736 | tf_op jit(solution)/shard_map/ppermute | solution.py:57
  4.0 22.8 %collective-permute-start.7 = (bf16[4,64,1024]{2,1,0:T(8,128)(2,1)S(1)}, bf16[4,64,1024]{2,1,0:T(8,128)(2,1)S(1)}, u32[]{:S(2)}, u32[]{:S(2)}) collective-permute-start(bf16[4,64,1024]{2,1,0:T(8,128)(2,1)S(1)} %constant_dynamic-slice_fusion), channel_id=1, source_target_pairs={{0,256},{1,257},{2,258},{3,259},{4,260},{5,261},{6,262},{7,263},{8... | collective-permute-start | bytes 1572872 | tf_op jit(solution)/shard_map/ppermute | solution.py:57
  10.9 45.1 %collective-permute-start.6 = (bf16[4,64,1024]{2,1,0:T(8,128)(2,1)S(1)}, bf16[4,64,1024]{2,1,0:T(8,128)(2,1)S(1)}, u32[]{:S(2)}, u32[]{:S(2)}) collective-permute-start(bf16[4,64,1024]{2,1,0:T(8,128)(2,1)S(1)} %constant_dynamic-slice_fusion), channel_id=1, source_target_pairs={{0,128},{1,129},{2,130},{3,131},{4,132},{5,133},{6,134},{7,135},{8... | collective-permute-start | bytes 1572872 | tf_op jit(solution)/shard_map/ppermute | solution.py:57
  12.8 43.1 %collective-permute-start.5 = (bf16[4,64,1024]{2,1,0:T(8,128)(2,1)S(1)}, bf16[4,64,1024]{2,1,0:T(8,128)(2,1)S(1)}, u32[]{:S(2)}, u32[]{:S(2)}) collective-permute-start(bf16[4,64,1024]{2,1,0:T(8,128)(2,1)S(1)} %constant_dynamic-slice_fusion), channel_id=1, source_target_pairs={{0,392},{1,393},{2,394},{3,395},{4,396},{5,397},{6,398},{7,399},{8... | collective-permute-start | bytes 1572872 | tf_op jit(solution)/shard_map/ppermute | solution.py:57
  16.2 62.3 %collective-permute-start.2 = (bf16[512,1024]{1,0:T(8,128)(2,1)}, bf16[512,1024]{1,0:T(8,128)(2,1)}, u32[]{:S(2)}, u32[]{:S(2)}) collective-permute-start(bf16[512,1024]{1,0:T(8,128)(2,1)} %bitcast.2.tok), channel_id=1, source_target_pairs={{1,0},{2,1},{3,2},{4,3},{5,4},{6,5},{7,6},{8,7},{9,8},{10,9},{11,1... | collective-permute-start | bytes 3145736 | tf_op jit(solution)/shard_map/ppermute | solution.py:57
  26.8 61.9 %collective-permute-start = (bf16[512,1024]{1,0:T(8,128)(2,1)}, bf16[512,1024]{1,0:T(8,128)(2,1)}, u32[]{:S(2)}, u32[]{:S(2)}) collective-permute-start(bf16[512,1024]{1,0:T(8,128)(2,1)} %bitcast.2.tok), channel_id=1, source_target_pairs={{0,1},{1,2},{2,3},{3,4},{4,5},{5,6},{6,7},{7,8},{8,9},{9,10},{10,1... | collective-permute-start | bytes 3145736 | tf_op jit(solution)/shard_map/ppermute | solution.py:57
  56.2 2.1 %copy-start = (bf16[3,4,64,1024]{3,2,1,0:T(8,128)(2,1)}, bf16[3,4,64,1024]{3,2,1,0:T(8,128)(2,1)S(1)}, u32[]{:S(2)}) copy-start(bf16[3,4,64,1024]{3,2,1,0:T(8,128)(2,1)S(1)} %pad_maximum_fusion.refs_2_) | copy-start | bytes 4718596
  56.2 62.7 %copy-start.4 = (s32[1,4,8]{2,1,0:T(4,128)S(1)}, s32[1,4,8]{2,1,0:T(4,128)}, u32[]{:S(2)}) copy-start(s32[1,4,8]{2,1,0:T(4,128)} %param.12) | copy-start | bytes 388
  56.3 34.3 %collective-permute-start.11 = (bf16[3,2,64,1024]{3,2,1,0:T(8,128)(2,1)S(1)}, bf16[3,2,64,1024]{3,2,1,0:T(8,128)(2,1)}, u32[]{:S(2)}, u32[]{:S(2)}) collective-permute-start(bf16[3,2,64,1024]{3,2,1,0:T(8,128)(2,1)S(1)} %get-tuple-element.13), channel_id=1, source_target_pairs={{0,16},{1,17},{2,18},{3,19},{4,20},{5,21},{6,22},{7,23},{8,24},{9,... | collective-permute-start | bytes 2359304 | tf_op jit(solution)/shard_map/ppermute | solution.py:57
  58.3 61.2 %collective-permute-start.9 = (bf16[3,4,64,1024]{3,2,1,0:T(8,128)(2,1)S(1)}, bf16[3,4,64,1024]{3,2,1,0:T(8,128)(2,1)}, u32[]{:S(2)}, u32[]{:S(2)}) collective-permute-start(bf16[3,4,64,1024]{3,2,1,0:T(8,128)(2,1)S(1)} %pad_maximum_fusion.refs_2_), channel_id=1, source_target_pairs={{0,64},{1,65},{2,66},{3,67},{4,68},{5,69},{6,70},{7,71},{8,72},{9,... | collective-permute-start | bytes 4718600 | tf_op jit(solution)/shard_map/ppermute | solution.py:57
  61.4 54.9 %collective-permute-start.8 = (bf16[3,2,64,1024]{3,2,1,0:T(8,128)(2,1)S(1)}, bf16[3,2,64,1024]{3,2,1,0:T(8,128)(2,1)S(1)}, u32[]{:S(2)}, u32[]{:S(2)}) collective-permute-start(bf16[3,2,64,1024]{3,2,1,0:T(8,128)(2,1)S(1)} %get-tuple-element.14), channel_id=1, source_target_pairs={{0,48},{1,49},{2,50},{3,51},{4,52},{5,53},{6,54},{7,55},{8,56},{9,... | collective-permute-start | bytes 2359304 | tf_op jit(solution)/shard_map/ppermute | solution.py:57
  78.6 66.3 %collective-permute-start.3 = (bf16[512,1024]{1,0:T(8,128)(2,1)}, bf16[512,1024]{1,0:T(8,128)(2,1)S(1)}, u32[]{:S(2)}, u32[]{:S(2)}) collective-permute-start(bf16[512,1024]{1,0:T(8,128)(2,1)} %collective-permute-done.2.tok), channel_id=1, source_target_pairs={{1,0},{2,1},{3,2},{4,3},{5,4},{6,5},{7,6},{8,7},{9,8},{10,9},{11,1... | collective-permute-start | bytes 3145736 | tf_op jit(solution)/shard_map/ppermute | solution.py:57
  88.7 56.2 %collective-permute-start.1 = (bf16[512,1024]{1,0:T(8,128)(2,1)}, bf16[512,1024]{1,0:T(8,128)(2,1)}, u32[]{:S(2)}, u32[]{:S(2)}) collective-permute-start(bf16[512,1024]{1,0:T(8,128)(2,1)} %collective-permute-done.tok), channel_id=1, source_target_pairs={{0,1},{1,2},{2,3},{3,4},{4,5},{5,6},{6,7},{7,8},{8,9},{9,10},{10,1... | collective-permute-start | bytes 3145736 | tf_op jit(solution)/shard_map/ppermute | solution.py:57
  90.6 28.8 %collective-permute-start.12 = (bf16[3,2,64,1024]{3,2,1,0:T(8,128)(2,1)}, bf16[3,2,64,1024]{3,2,1,0:T(8,128)(2,1)}, u32[]{:S(2)}, u32[]{:S(2)}) collective-permute-start(bf16[3,2,64,1024]{3,2,1,0:T(8,128)(2,1)} %collective-permute-done.11.refs_3_), channel_id=1, source_target_pairs={{0,64},{1,65},{2,66},{3,67},{4,68},{5,69},{6,70},{7,71},{8,72},{9,... | collective-permute-start | bytes 2359304 | tf_op jit(solution)/shard_map/ppermute | solution.py:57
  116.4 10.3 %copy-start.3 = (bf16[3,2,64,1024]{3,2,1,0:T(8,128)(2,1)}, bf16[3,2,64,1024]{3,2,1,0:T(8,128)(2,1)S(1)}, u32[]{:S(2)}) copy-start(bf16[3,2,64,1024]{3,2,1,0:T(8,128)(2,1)S(1)} %collective-permute-done.8.refs_3_) | copy-start | bytes 2359300
  116.4 22.7 %collective-permute-start.10 = (bf16[3,2,64,1024]{3,2,1,0:T(8,128)(2,1)S(1)}, bf16[3,2,64,1024]{3,2,1,0:T(8,128)(2,1)}, u32[]{:S(2)}, u32[]{:S(2)}) collective-permute-start(bf16[3,2,64,1024]{3,2,1,0:T(8,128)(2,1)S(1)} %collective-permute-done.8.refs_3_), channel_id=1, source_target_pairs={{0,64},{1,65},{2,66},{3,67},{4,68},{5,69},{6,70},{7,71},{8,72},{9,... | collective-permute-start | bytes 2359304 | tf_op jit(solution)/shard_map/ppermute | solution.py:57
  144.9 1.0 copy-start.2

commit v2 on v1

--- a/solution.py
+++ b/solution.py
@@ -105,8 +105,9 @@
     save.wait()
 
 
-def proj_kernel(tok, w, out):
-    out[...] = jnp.dot(normalise(tok[...]), w[...], preferred_element_type=F32).astype(BF)
+def pair_kernel(high, low, w, out):
+    tok = jnp.where(pl.program_id(0) < 2, high[...], low[...])
+    out[...] = jnp.dot(normalise(tok), w[...], preferred_element_type=F32).astype(BF)
 
 
 def query_kernel(pos, tok, *refs):
@@ -125,13 +126,14 @@
 
 
 def final_kernel(
-    idx, cnt, low2, up2, query, w_kv, w_o, kv_low, kv_own, kv_up, out, kv, w_buf, wo_buf, att, sem
+    idx, cnt, low2, up2, query, w_kv, w_o, kv_pair, kv_own, out, kv, w_buf, wo_buf, att, score, sem
 ):
     get_w = pltpu.make_async_copy(w_kv, w_buf, sem.at[0])
     get_w.start()
     gets = [
-        pltpu.make_async_copy(src, kv.at[pl.ds((i + 1) * ROWS, ROWS)], sem.at[1 + i])
-        for i, src in enumerate((kv_low, kv_own, kv_up))
+        pltpu.make_async_copy(kv_pair.at[pl.ds(ROWS, ROWS)], kv.at[pl.ds(ROWS, ROWS)], sem.at[1]),
+        pltpu.make_async_copy(kv_own, kv.at[pl.ds(2 * ROWS, ROWS)], sem.at[2]),
+        pltpu.make_async_copy(kv_pair.at[pl.ds(0, ROWS)], kv.at[pl.ds(3 * ROWS, ROWS)], sem.at[3]),
     ]
     gets.append(pltpu.make_async_copy(w_o, wo_buf, sem.at[4]))
     for g in gets:
@@ -148,34 +150,40 @@
     def one_block(b, carry):
         used = cnt[b]
         rows = pl.ds(pl.multiple_of(b * BLK, BLK), BLK)
-        starts = [pl.multiple_of(idx[b, j] * BLK, BLK) for j in range(MAXN)]
+        starts = [
+            pl.multiple_of(jnp.where(j < used, idx[b, j], idx[b, 0]) * BLK, BLK)
+            for j in range(MAXN)
+        ]
+        bias = [jnp.where(j < used, 0.0, -1e30) for j in range(MAXN)]
         for h in range(HEADS):
             hs = pl.ds(h * HD, HD)
             q = query[rows, hs]
-            scores = []
             for j in range(MAXN):
-                s = lax.dot_general(
+                score[h, :, j * BLK : (j + 1) * BLK] = lax.dot_general(
                     q, kv[pl.ds(starts[j], BLK), hs], (((1,), (1,)), ((), ())),
                     preferred_element_type=F32,
                 )
-                scores.append(jnp.where(j < used, s, -1e30))
+        for h in range(HEADS):
+            hs = pl.ds(h * HD, HD)
+            scores = [score[h, :, j * BLK : (j + 1) * BLK] for j in range(MAXN)]
             peak = scores[0]
             for s in scores[1:]:
                 peak = jnp.maximum(peak, s)
             peak = jnp.max(peak, axis=-1, keepdims=True)
-            expo = [jnp.exp2((s - peak) * SCALE2) for s in scores]
+            expo = [jnp.exp2((s - (peak - off)) * SCALE2) for s, off in zip(scores, bias)]
             total = expo[0]
             for e in expo[1:]:
                 total = total + e
             total = jnp.sum(total, axis=-1, keepdims=True)
-            acc = jnp.zeros((BLK, HD), F32)
+            acc = None
             for j in range(0, MAXN, 2):
                 vals = jnp.concatenate(
                     [kv[pl.ds(starts[i], BLK), pl.ds(D + h * HD, HD)] for i in (j, j + 1)], axis=0
                 )
                 wts = jnp.concatenate([expo[j].astype(BF), expo[j + 1].astype(BF)], axis=1)
-                acc = acc + jnp.dot(wts, vals, preferred_element_type=F32)
-            att[rows, hs] = (acc / total).astype(BF)
+                part = jnp.dot(wts, vals, preferred_element_type=F32)
+                acc = part if acc is None else acc + part
+            att[rows, hs] = (acc * (1.0 / total)).astype(BF)
         return carry
 
     lax.fori_loop(0, ROWS // BLK, one_block, 0)
@@ -230,22 +238,19 @@
         name="first_proj",
     )(pos, tok, *pieces_kv)
 
-    def project(t):
-        return pl.pallas_call(
-            proj_kernel,
-            grid=(2,),
-            in_specs=[
-                pl.BlockSpec((256, D), lambda i: (i, 0)),
-                pl.BlockSpec((D, 2 * D), lambda i: (0, 0), pipeline_mode=pl.Buffered(1)),
-            ],
-            out_specs=pl.BlockSpec((256, 2 * D), lambda i: (i, 0)),
-            out_shape=jax.ShapeDtypeStruct((ROWS, 2 * D), BF),
-            compiler_params=params,
-            name="proj",
-        )(t, w_kv)
-
-    kv_low = project(low)
-    kv_high = project(high)
+    kv_pair = pl.pallas_call(
+        pair_kernel,
+        grid=(4,),
+        in_specs=[
+            pl.BlockSpec((256, D), lambda i: (jnp.minimum(i, 1), 0)),
+            pl.BlockSpec((256, D), lambda i: (jnp.maximum(i - 2, 0), 0)),
+            pl.BlockSpec((D, 2 * D), lambda i: (0, 0), pipeline_mode=pl.Buffered(1)),
+        ],
+        out_specs=pl.BlockSpec((256, 2 * D), lambda i: (i, 0)),
+        out_shape=jax.ShapeDtypeStruct((2 * ROWS, 2 * D), BF),
+        compiler_params=params,
+        name="pair",
+    )(high, low, w_kv)
     query, w_o = pl.pallas_call(
         query_kernel,
         in_specs=[smem, vm] + [anyspace] * 6,
@@ -262,7 +267,7 @@
     index = nbr_index[0] - (rank * (ROWS // BLK) - REACH * (ROWS // BLK))
     update = pl.pallas_call(
         final_kernel,
-        in_specs=[smem, smem, vm, vm, vm] + [anyspace] * 5,
+        in_specs=[smem, smem, vm, vm, vm] + [anyspace] * 4,
         out_specs=vm,
         out_shape=jax.ShapeDtypeStruct((ROWS, D), BF),
         scratch_shapes=[
@@ -270,11 +275,12 @@
             pltpu.VMEM((D, 2 * D), BF),
             pltpu.VMEM((D, D), BF),
             pltpu.VMEM((ROWS, D), BF),
+            pltpu.VMEM((HEADS, BLK, MAXN * BLK), F32),
             pltpu.SemaphoreType.DMA((5,)),
         ],
         compiler_params=params,
         name="final",
-    )(index, nbr_count[0], low2, high2, query, w_kv, w_o, kv_low, kv_own, kv_high)
+    )(index, nbr_count[0], low2, high2, query, w_kv, w_o, kv_pair, kv_own)
     return update[None]
 
 

time: 173 us -> 165 us (0.954)
  Pallas kernels: 51.4 us -> 43.5 us
    pallas_call x1, Pallas kernels: 26 us -> 21.3 us  [body(): pl.pallas_call(final_kernel, in_specs=[smem, smem, vm, vm, vm] + [anyspac...]
    pallas_call x2 -> x1, Pallas kernels: 12.4 us -> 9.21 us  [body(): pl.pallas_call(pair_kernel, grid=(4,), in_specs=[pl.BlockSpec((256, D), l...]
  transfers between devices with their start and end apart: 13 -> 13, of which waited for: 2 -> 2; matrix products, arithmetic and copies ran while one was open for 1% -> 1% of each run, Pallas kernels for 15% -> 14%
where the time goes in v2:
time: 165 us; the launch traced here: 164 us
  starting transfers between devices  75.3 us (46%)
  Pallas kernels  43.5 us (26%)
  waiting for transfers between devices  40.9 us (25%)
  other arithmetic  2.74 us (2%)
    ppermute x13, starting transfers between devices, send(): return lax.ppermute(value, AXES, pairs)  75.3 us
    ppermute x13, waiting for transfers between devices, send(): return lax.ppermute(value, AXES, pairs)  40.9 us
    pallas_call x1, Pallas kernels, body(): pl.pallas_call(final_kernel, in_specs=[smem, smem, vm, vm, vm] + [anyspac...  21.3 us
    pallas_call x1, Pallas kernels, body(): pl.pallas_call(pair_kernel, grid=(4,), in_specs=[pl.BlockSpec((256, D), l...  9.21 us
    pallas_call x1, Pallas kernels, body(): pl.pallas_call(first_proj_kernel, in_specs=[smem, vm] + [anyspace] * 6, o...  7.18 us
    pallas_call x1, Pallas kernels, body(): pl.pallas_call(query_kernel, in_specs=[smem, vm] + [anyspace] * 6, out_sp...  5.77 us
  transfers between devices with their start and end apart: 13, of which 2 were waited for; matrix products, arithmetic and copies ran while one was open for 1% of the time, Pallas kernels for 14%

profile of v2, /device:TPU:49, one launch (start us, length us, event | category | flops | bytes accessed | tf_op | source)
XLA Modules:
  0.0 163.9 jit_solution(2855047064703372486)
XLA Ops:
  0.0 1.3 pad_maximum_fusion.1.refs_0_
  1.3 2.6 %collective-permute-start.4 = (bf16[4,128,1024]{2,1,0:T(8,128)(2,1)S(1)}, bf16[4,128,1024]{2,1,0:T(8,128)(2,1)}, u32[]{:S(2)}, u32[]{:S(2)}) collective-permute-start(bf16[4,128,1024]{2,1,0:T(8,128)(2,1)S(1)} %pad_maximum_fusion.1.refs_0_), channel_id=1, source_target_pairs={{0,64},{1,65},{2,66},{3,67},{4,68},{5,69},{6,70},{7,71},{8,72},{9,... | collective-permute-start | bytes 3145736 | tf_op jit(solution)/shard_map/ppermute | solution.py:57
  4.0 6.9 %collective-permute-start.7 = (bf16[4,64,1024]{2,1,0:T(8,128)(2,1)S(1)}, bf16[4,64,1024]{2,1,0:T(8,128)(2,1)S(1)}, u32[]{:S(2)}, u32[]{:S(2)}) collective-permute-start(bf16[4,64,1024]{2,1,0:T(8,128)(2,1)S(1)} %constant_dynamic-slice_fusion), channel_id=1, source_target_pairs={{0,256},{1,257},{2,258},{3,259},{4,260},{5,261},{6,262},{7,263},{8... | collective-permute-start | bytes 1572872 | tf_op jit(solution)/shard_map/ppermute | solution.py:57
  10.9 1.9 %collective-permute-start.6 = (bf16[4,64,1024]{2,1,0:T(8,128)(2,1)S(1)}, bf16[4,64,1024]{2,1,0:T(8,128)(2,1)S(1)}, u32[]{:S(2)}, u32[]{:S(2)}) collective-permute-start(bf16[4,64,1024]{2,1,0:T(8,128)(2,1)S(1)} %constant_dynamic-slice_fusion), channel_id=1, source_target_pairs={{0,128},{1,129},{2,130},{3,131},{4,132},{5,133},{6,134},{7,135},{8... | collective-permute-start | bytes 1572872 | tf_op jit(solution)/shard_map/ppermute | solution.py:57
  12.8 3.4 %collective-permute-start.5 = (bf16[4,64,1024]{2,1,0:T(8,128)(2,1)S(1)}, bf16[4,64,1024]{2,1,0:T(8,128)(2,1)S(1)}, u32[]{:S(2)}, u32[]{:S(2)}) collective-permute-start(bf16[4,64,1024]{2,1,0:T(8,128)(2,1)S(1)} %constant_dynamic-slice_fusion), channel_id=1, source_target_pairs={{0,392},{1,393},{2,394},{3,395},{4,396},{5,397},{6,398},{7,399},{8... | collective-permute-start | bytes 1572872 | tf_op jit(solution)/shard_map/ppermute | solution.py:57
  16.2 10.6 %collective-permute-start.2 = (bf16[512,1024]{1,0:T(8,128)(2,1)}, bf16[512,1024]{1,0:T(8,128)(2,1)}, u32[]{:S(2)}, u32[]{:S(2)}) collective-permute-start(bf16[512,1024]{1,0:T(8,128)(2,1)} %bitcast.2.tok), channel_id=1, source_target_pairs={{1,0},{2,1},{3,2},{4,3},{5,4},{6,5},{7,6},{8,7},{9,8},{10,9},{11,1... | collective-permute-start | bytes 3145736 | tf_op jit(solution)/shard_map/ppermute | solution.py:57
  26.8 1.9 %collective-permute-start = (bf16[512,1024]{1,0:T(8,128)(2,1)}, bf16[512,1024]{1,0:T(8,128)(2,1)}, u32[]{:S(2)}, u32[]{:S(2)}) collective-permute-start(bf16[512,1024]{1,0:T(8,128)(2,1)} %bitcast.2.tok), channel_id=1, source_target_pairs={{0,1},{1,2},{2,3},{3,4},{4,5},{5,6},{6,7},{7,8},{8,9},{9,10},{10,1... | collective-permute-start | bytes 3145736 | tf_op jit(solution)/shard_map/ppermute | solution.py:57
  28.7 27.3 %collective-permute-done.6 = bf16[4,64,1024]{2,1,0:T(8,128)(2,1)S(1)} collective-permute-done((bf16[4,64,1024]{2,1,0:T(8,128)(2,1)S(1)}, bf16[4,64,1024]{2,1,0:T(8,128)(2,1)S(1)}, u32[]{:S(2)}, u32[]{:S(2)}) %collective-permute-start.6) | collective-permute-done | bytes 524320 | tf_op jit(solution)/shard_map/ppermute | solution.py:57
  56.0 0.2 pad_maximum_fusion.refs_2_
  56.2 3.2 %collective-permute-start.9 = (bf16[3,4,64,1024]{3,2,1,0:T(8,128)(2,1)S(1)}, bf16[3,4,64,1024]{3,2,1,0:T(8,128)(2,1)}, u32[]{:S(2)}, u32[]{:S(2)}) collective-permute-start(bf16[3,4,64,1024]{3,2,1,0:T(8,128)(2,1)S(1)} %pad_maximum_fusion.refs_2_), channel_id=1, source_target_pairs={{0,64},{1,65},{2,66},{3,67},{4,68},{5,69},{6,70},{7,71},{8,72},{9,... | collective-permute-start | bytes 4718600 | tf_op jit(solution)/shard_map/ppermute | solution.py:57
  59.6 1.9 %collective-permute-start.8 = (bf16[3,2,64,1024]{3,2,1,0:T(8,128)(2,1)S(1)}, bf16[3,2,64,1024]{3,2,1,0:T(8,128)(2,1)}, u32[]{:S(2)}, u32[]{:S(2)}) collective-permute-start(bf16[3,2,64,1024]{3,2,1,0:T(8,128)(2,1)S(1)} %get-tuple-element.14), channel_id=1, source_target_pairs={{0,48},{1,49},{2,50},{3,51},{4,52},{5,53},{6,54},{7,55},{8,56},{9,... | collective-permute-start | bytes 2359304 | tf_op jit(solution)/shard_map/ppermute | solution.py:57
  61.5 3.4 %collective-permute-start.11 = (bf16[3,2,64,1024]{3,2,1,0:T(8,128)(2,1)S(1)}, bf16[3,2,64,1024]{3,2,1,0:T(8,128)(2,1)S(1)}, u32[]{:S(2)}, u32[]{:S(2)}) collective-permute-start(bf16[3,2,64,1024]{3,2,1,0:T(8,128)(2,1)S(1)} %get-tuple-element.13), channel_id=1, source_target_pairs={{0,16},{1,17},{2,18},{3,19},{4,20},{5,21},{6,22},{7,23},{8,24},{9,... | collective-permute-start | bytes 2359304 | tf_op jit(solution)/shard_map/ppermute | solution.py:57
  64.9 13.6 %collective-permute-done.2.high = bf16[512,1024]{1,0:T(8,128)(2,1)} collective-permute-done((bf16[512,1024]{1,0:T(8,128)(2,1)}, bf16[512,1024]{1,0:T(8,128)(2,1)}, u32[]{:S(2)}, u32[]{:S(2)}) %collective-permute-start.2) | collective-permute-done | bytes 1048608 | tf_op jit(solution)/shard_map/ppermute | solution.py:57
  78.6 10.1 %collective-permute-start.3 = (bf16[512,1024]{1,0:T(8,128)(2,1)}, bf16[512,1024]{1,0:T(8,128)(2,1)S(1)}, u32[]{:S(2)}, u32[]{:S(2)}) collective-permute-start(bf16[512,1024]{1,0:T(8,128)(2,1)} %collective-permute-done.2.high), channel_id=1, source_target_pairs={{1,0},{2,1},{3,2},{4,3},{5,4},{6,5},{7,6},{8,7},{9,8},{10,9},{11,1... | collective-permute-start | bytes 3145736 | tf_op jit(solution)/shard_map/ppermute | solution.py:57
  88.7 1.9 %collective-permute-start.1 = (bf16[512,1024]{1,0:T(8,128)(2,1)}, bf16[512,1024]{1,0:T(8,128)(2,1)}, u32[]{:S(2)}, u32[]{:S(2)}) collective-permute-start(bf16[512,1024]{1,0:T(8,128)(2,1)} %collective-permute-done.low), channel_id=1, source_target_pairs={{0,1},{1,2},{2,3},{3,4},{4,5},{5,6},{6,7},{7,8},{8,9},{9,10},{10,1... | collective-permute-start | bytes 3145736 | tf_op jit(solution)/shard_map/ppermute | solution.py:57
  90.6 25.6 %collective-permute-start.10 = (bf16[3,2,64,1024]{3,2,1,0:T(8,128)(2,1)}, bf16[3,2,64,1024]{3,2,1,0:T(8,128)(2,1)}, u32[]{:S(2)}, u32[]{:S(2)}) collective-permute-start(bf16[3,2,64,1024]{3,2,1,0:T(8,128)(2,1)} %collective-permute-done.8.refs_3_), channel_id=1, source_target_pairs={{0,64},{1,65},{2,66},{3,67},{4,68},{5,69},{6,70},{7,71},{8,72},{9,... | collective-permute-start | bytes 2359304 | tf_op jit(solution)/shard_map/ppermute | solution.py:57
  116.2 1.9 %collective-permute-start.12 = (bf16[3,2,64,1024]{3,2,1,0:T(8,128)(2,1)S(1)}, bf16[3,2,64,1024]{3,2,1,0:T(8,128)(2,1)}, u32[]{:S(2)}, u32[]{:S(2)}) collective-permute-start(bf16[3,2,64,1024]{3,2,1,0:T(8,128)(2,1)S(1)} %collective-permute-done.11.refs_3_), channel_id=1, source_target_pairs={{0,64},{1,65},{2,66},{3,67},{4,68},{5,69},{6,70},{7,71},{8,72},{9,... | collective-permute-start | bytes 2359304 | tf_op jit(solution)/shard_map/ppermute | solution.py:57
  118.2 0.7 pad_add_fusion.pos
  118.8 0.6 subtract_bitcast_fusion.idx
  119.4 5.8 %query.1 = (bf16[512,1024]{1,0:T(8,128)(2,1)}, bf16[1024,1024]{1,0:T(8,128)(2,1)}) custom-call(s32[3]{0:T(128)} %pad_add_fusion.pos, bf16[512,1024]{1,0:T(8,128)(2,1)} %bitcast.2.tok, bf16[4,128,1024]{2,1,0:T(8,128)(2,1)} %copy-done.1, bf16[4,128,1024]{2,1,0:T(8,128)(2,1)} %collective-permute-done.4.refs_1_, bf16[3,4,64,1024]{3,2,1,0:T(8,128)(2,1)} %copy-done, ...), custom_call_target="tpu_custom_call" | custom-call | tf_op jit(solution)/shard_map/query/pallas_call | solution.py:254
  125.2 7.2 %first_proj.1 = (bf16[512,2048]{1,0:T(8,128)(2,1)}, bf16[1024,2048]{1,0:T(8,128)(2,1)}) custom-call(s32[3]{0:T(128)} %pad_add_fusion.pos, bf16[512,1024]{1,0:T(8,128)(2,1)} %bitcast.2.tok, bf16[4,128,1024]{2,1,0:T(8,128)(2,1)} %copy-done.1, bf16[4,128,1024]{2,1,0:T(8,128)(2,1)} %collective-permute-done.4.refs_1_, bf16[3,4,64,1024]{3,2,1,0:T(8,128)(2,1)} %copy-done, ...), custom_call_target="tpu_custom_call" | custom-call | tf_op jit(solution)/shard_map/first_proj/pallas_call | solution.py:224
  132.4 9.2 %pair.1.kv_pair = bf16[1024,2048]{1,0:T(8,128)(2,1)} custom-call(bf16[512,1024]{1,0:T(8,128)(2,1)} %collective-permute-done.2.high, bf16[512,1024]{1,0:T(8,128)(2,1)} %collective-permute-done.low, bf16[1024,2048]{1,0:T(8,128)(2,1)} %get-tuple-element.10.w.w_kv), custom_call_target="tpu_custom_call" | custom-call | tf_op jit(solution)/shard_map/pair/pallas_call | solution.py:241
  141.7 1.0 copy-done.2
  142.6 21.3 %final.1 = bf16[512,1024]{1,0:T(8,128)(2,1)} custom-call(s32[4,8]{1,0:T(4,128)} %subtract_bitcast_fusion.idx, s32[4]{0:T(128)} %bitcast.22, bf16[512,1024]{1,0:T(8,128)(2,1)} %collective-permute-done.1.low2, bf16[512,1024]{1,0:T(8,128)(2,1)} %copy-done.2, bf16[512,1024]{1,0:T(8,128)(2,1)} %get-tuple-element.9.query, ...), custom_call_target="tpu_custom_call" | custom-call | tf_op jit(solution)/shard_map/final/pallas_call | solution.py:268
  (22 shorter events, 0.2 us)
Async XLA Ops:
  1.3 54.8 %copy-start.1 = (bf16[4,128,1024]{2,1,0:T(8,128)(2,1)}, bf16[4,128,1024]{2,1,0:T(8,128)(2,1)S(1)}, u32[]{:S(2)}) copy-start(bf16[4,128,1024]{2,1,0:T(8,128)(2,1)S(1)} %pad_maximum_fusion.1.refs_0_) | copy-start | bytes 3145732
  1.3 60.2 %collective-permute-start.4 = (bf16[4,128,1024]{2,1,0:T(8,128)(2,1)S(1)}, bf16[4,128,1024]{2,1,0:T(8,128)(2,1)}, u32[]{:S(2)}, u32[]{:S(2)}) collective-permute-start(bf16[4,128,1024]{2,1,0:T(8,128)(2,1)S(1)} %pad_maximum_fusion.1.refs_0_), channel_id=1, source_target_pairs={{0,64},{1,65},{2,66},{3,67},{4,68},{5,69},{6,70},{7,71},{8,72},{9,... | collective-permute-start | bytes 3145736 | tf_op jit(solution)/shard_map/ppermute | solution.py:57
  4.0 22.8 %collective-permute-start.7 = (bf16[4,64,1024]{2,1,0:T(8,128)(2,1)S(1)}, bf16[4,64,1024]{2,1,0:T(8,128)(2,1)S(1)}, u32[]{:S(2)}, u32[]{:S(2)}) collective-permute-start(bf16[4,64,1024]{2,1,0:T(8,128)(2,1)S(1)} %constant_dynamic-slice_fusion), channel_id=1, source_target_pairs={{0,256},{1,257},{2,258},{3,259},{4,260},{5,261},{6,262},{7,263},{8... | collective-permute-start | bytes 1572872 | tf_op jit(solution)/shard_map/ppermute | solution.py:57
  10.9 45.1 %collective-permute-start.6 = (bf16[4,64,1024]{2,1,0:T(8,128)(2,1)S(1)}, bf16[4,64,1024]{2,1,0:T(8,128)(2,1)S(1)}, u32[]{:S(2)}, u32[]{:S(2)}) collective-permute-start(bf16[4,64,1024]{2,1,0:T(8,128)(2,1)S(1)} %constant_dynamic-slice_fusion), channel_id=1, source_target_pairs={{0,128},{1,129},{2,130},{3,131},{4,132},{5,133},{6,134},{7,135},{8... | collective-permute-start | bytes 1572872 | tf_op jit(solution)/shard_map/ppermute | solution.py:57
  12.8 43.1 %collective-permute-start.5 = (bf16[4,64,1024]{2,1,0:T(8,128)(2,1)S(1)}, bf16[4,64,1024]{2,1,0:T(8,128)(2,1)S(1)}, u32[]{:S(2)}, u32[]{:S(2)}) collective-permute-start(bf16[4,64,1024]{2,1,0:T(8,128)(2,1)S(1)} %constant_dynamic-slice_fusion), channel_id=1, source_target_pairs={{0,392},{1,393},{2,394},{3,395},{4,396},{5,397},{6,398},{7,399},{8... | collective-permute-start | bytes 1572872 | tf_op jit(solution)/shard_map/ppermute | solution.py:57
  16.2 62.3 %collective-permute-start.2 = (bf16[512,1024]{1,0:T(8,128)(2,1)}, bf16[512,1024]{1,0:T(8,128)(2,1)}, u32[]{:S(2)}, u32[]{:S(2)}) collective-permute-start(bf16[512,1024]{1,0:T(8,128)(2,1)} %bitcast.2.tok), channel_id=1, source_target_pairs={{1,0},{2,1},{3,2},{4,3},{5,4},{6,5},{7,6},{8,7},{9,8},{10,9},{11,1... | collective-permute-start | bytes 3145736 | tf_op jit(solution)/shard_map/ppermute | solution.py:57
  26.8 61.9 %collective-permute-start = (bf16[512,1024]{1,0:T(8,128)(2,1)}, bf16[512,1024]{1,0:T(8,128)(2,1)}, u32[]{:S(2)}, u32[]{:S(2)}) collective-permute-start(bf16[512,1024]{1,0:T(8,128)(2,1)} %bitcast.2.tok), channel_id=1, source_target_pairs={{0,1},{1,2},{2,3},{3,4},{4,5},{5,6},{6,7},{7,8},{8,9},{9,10},{10,1... | collective-permute-start | bytes 3145736 | tf_op jit(solution)/shard_map/ppermute | solution.py:57
  56.2 3.4 %copy-start = (bf16[3,4,64,1024]{3,2,1,0:T(8,128)(2,1)}, bf16[3,4,64,1024]{3,2,1,0:T(8,128)(2,1)S(1)}, u32[]{:S(2)}) copy-start(bf16[3,4,64,1024]{3,2,1,0:T(8,128)(2,1)S(1)} %pad_maximum_fusion.refs_2_) | copy-start | bytes 4718596
  56.2 62.7 %copy-start.4 = (s32[1,4,8]{2,1,0:T(4,128)S(1)}, s32[1,4,8]{2,1,0:T(4,128)}, u32[]{:S(2)}) copy-start(s32[1,4,8]{2,1,0:T(4,128)} %param.12) | copy-start | bytes 388
  56.2 63.3 %collective-permute-start.9 = (bf16[3,4,64,1024]{3,2,1,0:T(8,128)(2,1)S(1)}, bf16[3,4,64,1024]{3,2,1,0:T(8,128)(2,1)}, u32[]{:S(2)}, u32[]{:S(2)}) collective-permute-start(bf16[3,4,64,1024]{3,2,1,0:T(8,128)(2,1)S(1)} %pad_maximum_fusion.refs_2_), channel_id=1, source_target_pairs={{0,64},{1,65},{2,66},{3,67},{4,68},{5,69},{6,70},{7,71},{8,72},{9,... | collective-permute-start | bytes 4718600 | tf_op jit(solution)/shard_map/ppermute | solution.py:57
  59.6 31.0 %collective-permute-start.8 = (bf16[3,2,64,1024]{3,2,1,0:T(8,128)(2,1)S(1)}, bf16[3,2,64,1024]{3,2,1,0:T(8,128)(2,1)}, u32[]{:S(2)}, u32[]{:S(2)}) collective-permute-start(bf16[3,2,64,1024]{3,2,1,0:T(8,128)(2,1)S(1)} %get-tuple-element.14), channel_id=1, source_target_pairs={{0,48},{1,49},{2,50},{3,51},{4,52},{5,53},{6,54},{7,55},{8,56},{9,... | collective-permute-start | bytes 2359304 | tf_op jit(solution)/shard_map/ppermute | solution.py:57
  61.5 54.7 %collective-permute-start.11 = (bf16[3,2,64,1024]{3,2,1,0:T(8,128)(2,1)S(1)}, bf16[3,2,64,1024]{3,2,1,0:T(8,128)(2,1)S(1)}, u32[]{:S(2)}, u32[]{:S(2)}) collective-permute-start(bf16[3,2,64,1024]{3,2,1,0:T(8,128)(2,1)S(1)} %get-tuple-element.13), channel_id=1, source_target_pairs={{0,16},{1,17},{2,18},{3,19},{4,20},{5,21},{6,22},{7,23},{8,24},{9,... | collective-permute-start | bytes 2359304 | tf_op jit(solution)/shard_map/ppermute | solution.py:57
  78.6 63.1 %collective-permute-start.3 = (bf16[512,1024]{1,0:T(8,128)(2,1)}, bf16[512,1024]{1,0:T(8,128)(2,1)S(1)}, u32[]{:S(2)}, u32[]{:S(2)}) collective-permute-start(bf16[512,1024]{1,0:T(8,128)(2,1)} %collective-permute-done.2.high), channel_id=1, source_target_pairs={{1,0},{2,1},{3,2},{4,3},{5,4},{6,5},{7,6},{8,7},{9,8},{10,9},{11,1... | collective-permute-start | bytes 3145736 | tf_op jit(solution)/shard_map/ppermute | solution.py:57
  88.7 53.0 %collective-permute-start.1 = (bf16[512,1024]{1,0:T(8,128)(2,1)}, bf16[512,1024]{1,0:T(8,128)(2,1)}, u32[]{:S(2)}, u32[]{:S(2)}) collective-permute-start(bf16[512,1024]{1,0:T(8,128)(2,1)} %collective-permute-done.low), channel_id=1, source_target_pairs={{0,1},{1,2},{2,3},{3,4},{4,5},{5,6},{6,7},{7,8},{8,9},{9,10},{10,1... | collective-permute-start | bytes 3145736 | tf_op jit(solution)/shard_map/ppermute | solution.py:57
  90.6 28.8 %collective-permute-start.10 = (bf16[3,2,64,1024]{3,2,1,0:T(8,128)(2,1)}, bf16[3,2,64,1024]{3,2,1,0:T(8,128)(2,1)}, u32[]{:S(2)}, u32[]{:S(2)}) collective-permute-start(bf16[3,2,64,1024]{3,2,1,0:T(8,128)(2,1)} %collective-permute-done.8.refs_3_), channel_id=1, source_target_pairs={{0,64},{1,65},{2,66},{3,67},{4,68},{5,69},{6,70},{7,71},{8,72},{9,... | collective-permute-start | bytes 2359304 | tf_op jit(solution)/shard_map/ppermute | solution.py:57
  116.2 9.0 %copy-start.3 = (bf16[3,2,64,1024]{3,2,1,0:T(8,128)(2,1)}, bf16[3,2,64,1024]{3,2,1,0:T(8,128)(2,1)S(1)}, u32[]{:S(2)}) copy-start(bf16[3,2,64,1024]{3,2,1,0:T(8,128)(2,1)S(1)} %collective-permute-done.11.refs_3_) | copy-start | bytes 2359300
  116.2 9.0 %collective-permute-start.12 = (bf16[3,2,64,1024]{3,2,1,0:T(8,128)(2,1)S(1)}, bf16[3,2,64,1024]{3,2,1,0:T(8,128)(2,1)}, u32[]{:S(2)}, u32[]{:S(2)}) collective-permute-start(bf16[3,2,64,1024]{3,2,1,0:T(8,128)(2,1)S(1)} %collective-permute-done.11.refs_3_), channel_id=1, source_target_pairs={{0,64},{1,65},{2,66},{3,67},{4,68},{5,69},{6,70},{7,71},{8,72},{9,... | collective-permute-start | bytes 2359304 | tf_op jit(solution)/shard_map/ppermute | solution.py:57
  141.7 1.0 copy-start.2

commit v3 on v2

--- a/solution.py
+++ b/solution.py
@@ -93,15 +93,12 @@
     copies = piece_copies(pos, srcs, (0, 1), w_buf, sem)
     for c in copies:
         c.start()
+    normed = normalise(tok[...])
     for c in copies:
         c.wait()
     save = pltpu.make_async_copy(w_buf, w_out, sem2)
     save.start()
-    for i in range(0, ROWS, 256):
-        rows = slice(i, i + 256)
-        out[rows, :] = jnp.dot(
-            normalise(tok[rows, :]), w_buf[...], preferred_element_type=F32
-        ).astype(BF)
+    out[...] = jnp.dot(normed, w_buf[...], preferred_element_type=F32).astype(BF)
     save.wait()
 
 
@@ -115,13 +112,12 @@
     copies = piece_copies(pos, srcs, (2, 3), w_buf, sem)
     for c in copies:
         c.start()
+    normed = normalise(tok[...])
     for c in copies:
         c.wait()
     save = pltpu.make_async_copy(w_buf.at[:, pl.ds(D, D)], w_out, sem2)
     save.start()
-    out[...] = jnp.dot(
-        normalise(tok[...]), w_buf[:, :D], preferred_element_type=F32
-    ).astype(BF)
+    out[...] = jnp.dot(normed, w_buf[:, :D], preferred_element_type=F32).astype(BF)
     save.wait()
 
 
@@ -138,12 +134,12 @@
     gets.append(pltpu.make_async_copy(w_o, wo_buf, sem.at[4]))
     for g in gets:
         g.start()
+    normed = [normalise(low2[...]), normalise(up2[...])]
     get_w.wait()
-    for tok, base in ((low2, 0), (up2, 4 * ROWS)):
-        for i in range(0, ROWS, 256):
-            kv[base + i : base + i + 256, :] = jnp.dot(
-                normalise(tok[i : i + 256, :]), w_buf[...], preferred_element_type=F32
-            ).astype(BF)
+    for tok, base in zip(normed, (0, 4 * ROWS)):
+        kv[base : base + ROWS, :] = jnp.dot(
+            tok, w_buf[...], preferred_element_type=F32
+        ).astype(BF)
     for g in gets:
         g.wait()
 

time: 165 us -> 164 us (level)
  transfers between devices with their start and end apart: 13 -> 13, of which waited for: 2 -> 2; matrix products, arithmetic and copies ran while one was open for 1% -> 1% of each run, Pallas kernels for 14% -> 13%
where the time goes in v3:
time: 164 us
  starting transfers between devices  75.3 us (46%)
  Pallas kernels  43.2 us (26%)
  waiting for transfers between devices  40.9 us (25%)
  other arithmetic  2.74 us (2%)
    ppermute x13, starting transfers between devices, send(): return lax.ppermute(value, AXES, pairs)  75.3 us
    ppermute x13, waiting for transfers between devices, send(): return lax.ppermute(value, AXES, pairs)  40.9 us
    pallas_call x1, Pallas kernels, body(): pl.pallas_call(final_kernel, in_specs=[smem, smem, vm, vm, vm] + [anyspac...  21.2 us
    pallas_call x1, Pallas kernels, body(): pl.pallas_call(pair_kernel, grid=(4,), in_specs=[pl.BlockSpec((256, D), l...  9.21 us
    pallas_call x1, Pallas kernels, body(): pl.pallas_call(first_proj_kernel, in_specs=[smem, vm] + [anyspace] * 6, o...  7.06 us
    pallas_call x1, Pallas kernels, body(): pl.pallas_call(query_kernel, in_specs=[smem, vm] + [anyspace] * 6, out_sp...  5.74 us
  transfers between devices with their start and end apart: 13, of which 2 were waited for; matrix products, arithmetic and copies ran while one was open for 1% of the time, Pallas kernels for 13%

profile of v3, /device:TPU:49, one launch (start us, length us, event | category | flops | bytes accessed | tf_op | source)
XLA Modules:
  0.0 163.7 jit_solution(6215301621388338205)
XLA Ops:
  0.0 1.3 pad_maximum_fusion.1.refs_0_
  1.3 2.6 %collective-permute-start.4 = (bf16[4,128,1024]{2,1,0:T(8,128)(2,1)S(1)}, bf16[4,128,1024]{2,1,0:T(8,128)(2,1)}, u32[]{:S(2)}, u32[]{:S(2)}) collective-permute-start(bf16[4,128,1024]{2,1,0:T(8,128)(2,1)S(1)} %pad_maximum_fusion.1.refs_0_), channel_id=1, source_target_pairs={{0,64},{1,65},{2,66},{3,67},{4,68},{5,69},{6,70},{7,71},{8,72},{9,... | collective-permute-start | bytes 3145736 | tf_op jit(solution)/shard_map/ppermute | solution.py:57
  4.0 6.9 %collective-permute-start.7 = (bf16[4,64,1024]{2,1,0:T(8,128)(2,1)S(1)}, bf16[4,64,1024]{2,1,0:T(8,128)(2,1)S(1)}, u32[]{:S(2)}, u32[]{:S(2)}) collective-permute-start(bf16[4,64,1024]{2,1,0:T(8,128)(2,1)S(1)} %constant_dynamic-slice_fusion), channel_id=1, source_target_pairs={{0,256},{1,257},{2,258},{3,259},{4,260},{5,261},{6,262},{7,263},{8... | collective-permute-start | bytes 1572872 | tf_op jit(solution)/shard_map/ppermute | solution.py:57
  10.9 1.9 %collective-permute-start.6 = (bf16[4,64,1024]{2,1,0:T(8,128)(2,1)S(1)}, bf16[4,64,1024]{2,1,0:T(8,128)(2,1)S(1)}, u32[]{:S(2)}, u32[]{:S(2)}) collective-permute-start(bf16[4,64,1024]{2,1,0:T(8,128)(2,1)S(1)} %constant_dynamic-slice_fusion), channel_id=1, source_target_pairs={{0,128},{1,129},{2,130},{3,131},{4,132},{5,133},{6,134},{7,135},{8... | collective-permute-start | bytes 1572872 | tf_op jit(solution)/shard_map/ppermute | solution.py:57
  12.8 3.4 %collective-permute-start.5 = (bf16[4,64,1024]{2,1,0:T(8,128)(2,1)S(1)}, bf16[4,64,1024]{2,1,0:T(8,128)(2,1)S(1)}, u32[]{:S(2)}, u32[]{:S(2)}) collective-permute-start(bf16[4,64,1024]{2,1,0:T(8,128)(2,1)S(1)} %constant_dynamic-slice_fusion), channel_id=1, source_target_pairs={{0,392},{1,393},{2,394},{3,395},{4,396},{5,397},{6,398},{7,399},{8... | collective-permute-start | bytes 1572872 | tf_op jit(solution)/shard_map/ppermute | solution.py:57
  16.2 10.6 %collective-permute-start.2 = (bf16[512,1024]{1,0:T(8,128)(2,1)}, bf16[512,1024]{1,0:T(8,128)(2,1)}, u32[]{:S(2)}, u32[]{:S(2)}) collective-permute-start(bf16[512,1024]{1,0:T(8,128)(2,1)} %bitcast.2.tok), channel_id=1, source_target_pairs={{1,0},{2,1},{3,2},{4,3},{5,4},{6,5},{7,6},{8,7},{9,8},{10,9},{11,1... | collective-permute-start | bytes 3145736 | tf_op jit(solution)/shard_map/ppermute | solution.py:57
  26.8 1.9 %collective-permute-start = (bf16[512,1024]{1,0:T(8,128)(2,1)}, bf16[512,1024]{1,0:T(8,128)(2,1)}, u32[]{:S(2)}, u32[]{:S(2)}) collective-permute-start(bf16[512,1024]{1,0:T(8,128)(2,1)} %bitcast.2.tok), channel_id=1, source_target_pairs={{0,1},{1,2},{2,3},{3,4},{4,5},{5,6},{6,7},{7,8},{8,9},{9,10},{10,1... | collective-permute-start | bytes 3145736 | tf_op jit(solution)/shard_map/ppermute | solution.py:57
  28.7 27.3 %collective-permute-done.6 = bf16[4,64,1024]{2,1,0:T(8,128)(2,1)S(1)} collective-permute-done((bf16[4,64,1024]{2,1,0:T(8,128)(2,1)S(1)}, bf16[4,64,1024]{2,1,0:T(8,128)(2,1)S(1)}, u32[]{:S(2)}, u32[]{:S(2)}) %collective-permute-start.6) | collective-permute-done | bytes 524320 | tf_op jit(solution)/shard_map/ppermute | solution.py:57
  56.0 0.2 pad_maximum_fusion.refs_2_
  56.2 3.2 %collective-permute-start.9 = (bf16[3,4,64,1024]{3,2,1,0:T(8,128)(2,1)S(1)}, bf16[3,4,64,1024]{3,2,1,0:T(8,128)(2,1)}, u32[]{:S(2)}, u32[]{:S(2)}) collective-permute-start(bf16[3,4,64,1024]{3,2,1,0:T(8,128)(2,1)S(1)} %pad_maximum_fusion.refs_2_), channel_id=1, source_target_pairs={{0,64},{1,65},{2,66},{3,67},{4,68},{5,69},{6,70},{7,71},{8,72},{9,... | collective-permute-start | bytes 4718600 | tf_op jit(solution)/shard_map/ppermute | solution.py:57
  59.6 1.9 %collective-permute-start.8 = (bf16[3,2,64,1024]{3,2,1,0:T(8,128)(2,1)S(1)}, bf16[3,2,64,1024]{3,2,1,0:T(8,128)(2,1)}, u32[]{:S(2)}, u32[]{:S(2)}) collective-permute-start(bf16[3,2,64,1024]{3,2,1,0:T(8,128)(2,1)S(1)} %get-tuple-element.14), channel_id=1, source_target_pairs={{0,48},{1,49},{2,50},{3,51},{4,52},{5,53},{6,54},{7,55},{8,56},{9,... | collective-permute-start | bytes 2359304 | tf_op jit(solution)/shard_map/ppermute | solution.py:57
  61.5 3.4 %collective-permute-start.11 = (bf16[3,2,64,1024]{3,2,1,0:T(8,128)(2,1)S(1)}, bf16[3,2,64,1024]{3,2,1,0:T(8,128)(2,1)S(1)}, u32[]{:S(2)}, u32[]{:S(2)}) collective-permute-start(bf16[3,2,64,1024]{3,2,1,0:T(8,128)(2,1)S(1)} %get-tuple-element.13), channel_id=1, source_target_pairs={{0,16},{1,17},{2,18},{3,19},{4,20},{5,21},{6,22},{7,23},{8,24},{9,... | collective-permute-start | bytes 2359304 | tf_op jit(solution)/shard_map/ppermute | solution.py:57
  64.9 13.6 %collective-permute-done.2.high = bf16[512,1024]{1,0:T(8,128)(2,1)} collective-permute-done((bf16[512,1024]{1,0:T(8,128)(2,1)}, bf16[512,1024]{1,0:T(8,128)(2,1)}, u32[]{:S(2)}, u32[]{:S(2)}) %collective-permute-start.2) | collective-permute-done | bytes 1048608 | tf_op jit(solution)/shard_map/ppermute | solution.py:57
  78.6 10.1 %collective-permute-start.3 = (bf16[512,1024]{1,0:T(8,128)(2,1)}, bf16[512,1024]{1,0:T(8,128)(2,1)S(1)}, u32[]{:S(2)}, u32[]{:S(2)}) collective-permute-start(bf16[512,1024]{1,0:T(8,128)(2,1)} %collective-permute-done.2.high), channel_id=1, source_target_pairs={{1,0},{2,1},{3,2},{4,3},{5,4},{6,5},{7,6},{8,7},{9,8},{10,9},{11,1... | collective-permute-start | bytes 3145736 | tf_op jit(solution)/shard_map/ppermute | solution.py:57
  88.7 1.9 %collective-permute-start.1 = (bf16[512,1024]{1,0:T(8,128)(2,1)}, bf16[512,1024]{1,0:T(8,128)(2,1)}, u32[]{:S(2)}, u32[]{:S(2)}) collective-permute-start(bf16[512,1024]{1,0:T(8,128)(2,1)} %collective-permute-done.low), channel_id=1, source_target_pairs={{0,1},{1,2},{2,3},{3,4},{4,5},{5,6},{6,7},{7,8},{8,9},{9,10},{10,1... | collective-permute-start | bytes 3145736 | tf_op jit(solution)/shard_map/ppermute | solution.py:57
  90.6 25.6 %collective-permute-start.10 = (bf16[3,2,64,1024]{3,2,1,0:T(8,128)(2,1)}, bf16[3,2,64,1024]{3,2,1,0:T(8,128)(2,1)}, u32[]{:S(2)}, u32[]{:S(2)}) collective-permute-start(bf16[3,2,64,1024]{3,2,1,0:T(8,128)(2,1)} %collective-permute-done.8.refs_3_), channel_id=1, source_target_pairs={{0,64},{1,65},{2,66},{3,67},{4,68},{5,69},{6,70},{7,71},{8,72},{9,... | collective-permute-start | bytes 2359304 | tf_op jit(solution)/shard_map/ppermute | solution.py:57
  116.2 1.9 %collective-permute-start.12 = (bf16[3,2,64,1024]{3,2,1,0:T(8,128)(2,1)S(1)}, bf16[3,2,64,1024]{3,2,1,0:T(8,128)(2,1)}, u32[]{:S(2)}, u32[]{:S(2)}) collective-permute-start(bf16[3,2,64,1024]{3,2,1,0:T(8,128)(2,1)S(1)} %collective-permute-done.11.refs_3_), channel_id=1, source_target_pairs={{0,64},{1,65},{2,66},{3,67},{4,68},{5,69},{6,70},{7,71},{8,72},{9,... | collective-permute-start | bytes 2359304 | tf_op jit(solution)/shard_map/ppermute | solution.py:57
  118.2 0.7 pad_add_fusion.pos
  118.8 0.6 subtract_bitcast_fusion.idx
  119.4 5.7 %query.1 = (bf16[512,1024]{1,0:T(8,128)(2,1)}, bf16[1024,1024]{1,0:T(8,128)(2,1)}) custom-call(s32[3]{0:T(128)} %pad_add_fusion.pos, bf16[512,1024]{1,0:T(8,128)(2,1)} %bitcast.2.tok, bf16[4,128,1024]{2,1,0:T(8,128)(2,1)} %copy-done.1, bf16[4,128,1024]{2,1,0:T(8,128)(2,1)} %collective-permute-done.4.refs_1_, bf16[3,4,64,1024]{3,2,1,0:T(8,128)(2,1)} %copy-done, ...), custom_call_target="tpu_custom_call" | custom-call | tf_op jit(solution)/shard_map/query/pallas_call | solution.py:250
  125.2 7.1 %first_proj.1 = (bf16[512,2048]{1,0:T(8,128)(2,1)}, bf16[1024,2048]{1,0:T(8,128)(2,1)}) custom-call(s32[3]{0:T(128)} %pad_add_fusion.pos, bf16[512,1024]{1,0:T(8,128)(2,1)} %bitcast.2.tok, bf16[4,128,1024]{2,1,0:T(8,128)(2,1)} %copy-done.1, bf16[4,128,1024]{2,1,0:T(8,128)(2,1)} %collective-permute-done.4.refs_1_, bf16[3,4,64,1024]{3,2,1,0:T(8,128)(2,1)} %copy-done, ...), custom_call_target="tpu_custom_call" | custom-call | tf_op jit(solution)/shard_map/first_proj/pallas_call | solution.py:220
  132.3 9.2 %pair.1.kv_pair = bf16[1024,2048]{1,0:T(8,128)(2,1)} custom-call(bf16[512,1024]{1,0:T(8,128)(2,1)} %collective-permute-done.2.high, bf16[512,1024]{1,0:T(8,128)(2,1)} %collective-permute-done.low, bf16[1024,2048]{1,0:T(8,128)(2,1)} %get-tuple-element.10.w.w_kv), custom_call_target="tpu_custom_call" | custom-call | tf_op jit(solution)/shard_map/pair/pallas_call | solution.py:237
  141.5 1.0 copy-done.2
  142.5 21.2 %final.1 = bf16[512,1024]{1,0:T(8,128)(2,1)} custom-call(s32[4,8]{1,0:T(4,128)} %subtract_bitcast_fusion.idx, s32[4]{0:T(128)} %bitcast.22, bf16[512,1024]{1,0:T(8,128)(2,1)} %collective-permute-done.1.low2, bf16[512,1024]{1,0:T(8,128)(2,1)} %copy-done.2, bf16[512,1024]{1,0:T(8,128)(2,1)} %get-tuple-element.9.query, ...), custom_call_target="tpu_custom_call" | custom-call | tf_op jit(solution)/shard_map/final/pallas_call | solution.py:264
  (22 shorter events, 0.2 us)
Async XLA Ops:
  1.3 54.8 %copy-start.1 = (bf16[4,128,1024]{2,1,0:T(8,128)(2,1)}, bf16[4,128,1024]{2,1,0:T(8,128)(2,1)S(1)}, u32[]{:S(2)}) copy-start(bf16[4,128,1024]{2,1,0:T(8,128)(2,1)S(1)} %pad_maximum_fusion.1.refs_0_) | copy-start | bytes 3145732
  1.3 60.2 %collective-permute-start.4 = (bf16[4,128,1024]{2,1,0:T(8,128)(2,1)S(1)}, bf16[4,128,1024]{2,1,0:T(8,128)(2,1)}, u32[]{:S(2)}, u32[]{:S(2)}) collective-permute-start(bf16[4,128,1024]{2,1,0:T(8,128)(2,1)S(1)} %pad_maximum_fusion.1.refs_0_), channel_id=1, source_target_pairs={{0,64},{1,65},{2,66},{3,67},{4,68},{5,69},{6,70},{7,71},{8,72},{9,... | collective-permute-start | bytes 3145736 | tf_op jit(solution)/shard_map/ppermute | solution.py:57
  4.0 22.8 %collective-permute-start.7 = (bf16[4,64,1024]{2,1,0:T(8,128)(2,1)S(1)}, bf16[4,64,1024]{2,1,0:T(8,128)(2,1)S(1)}, u32[]{:S(2)}, u32[]{:S(2)}) collective-permute-start(bf16[4,64,1024]{2,1,0:T(8,128)(2,1)S(1)} %constant_dynamic-slice_fusion), channel_id=1, source_target_pairs={{0,256},{1,257},{2,258},{3,259},{4,260},{5,261},{6,262},{7,263},{8... | collective-permute-start | bytes 1572872 | tf_op jit(solution)/shard_map/ppermute | solution.py:57
  10.9 45.1 %collective-permute-start.6 = (bf16[4,64,1024]{2,1,0:T(8,128)(2,1)S(1)}, bf16[4,64,1024]{2,1,0:T(8,128)(2,1)S(1)}, u32[]{:S(2)}, u32[]{:S(2)}) collective-permute-start(bf16[4,64,1024]{2,1,0:T(8,128)(2,1)S(1)} %constant_dynamic-slice_fusion), channel_id=1, source_target_pairs={{0,128},{1,129},{2,130},{3,131},{4,132},{5,133},{6,134},{7,135},{8... | collective-permute-start | bytes 1572872 | tf_op jit(solution)/shard_map/ppermute | solution.py:57
  12.8 43.1 %collective-permute-start.5 = (bf16[4,64,1024]{2,1,0:T(8,128)(2,1)S(1)}, bf16[4,64,1024]{2,1,0:T(8,128)(2,1)S(1)}, u32[]{:S(2)}, u32[]{:S(2)}) collective-permute-start(bf16[4,64,1024]{2,1,0:T(8,128)(2,1)S(1)} %constant_dynamic-slice_fusion), channel_id=1, source_target_pairs={{0,392},{1,393},{2,394},{3,395},{4,396},{5,397},{6,398},{7,399},{8... | collective-permute-start | bytes 1572872 | tf_op jit(solution)/shard_map/ppermute | solution.py:57
  16.2 62.3 %collective-permute-start.2 = (bf16[512,1024]{1,0:T(8,128)(2,1)}, bf16[512,1024]{1,0:T(8,128)(2,1)}, u32[]{:S(2)}, u32[]{:S(2)}) collective-permute-start(bf16[512,1024]{1,0:T(8,128)(2,1)} %bitcast.2.tok), channel_id=1, source_target_pairs={{1,0},{2,1},{3,2},{4,3},{5,4},{6,5},{7,6},{8,7},{9,8},{10,9},{11,1... | collective-permute-start | bytes 3145736 | tf_op jit(solution)/shard_map/ppermute | solution.py:57
  26.8 61.9 %collective-permute-start = (bf16[512,1024]{1,0:T(8,128)(2,1)}, bf16[512,1024]{1,0:T(8,128)(2,1)}, u32[]{:S(2)}, u32[]{:S(2)}) collective-permute-start(bf16[512,1024]{1,0:T(8,128)(2,1)} %bitcast.2.tok), channel_id=1, source_target_pairs={{0,1},{1,2},{2,3},{3,4},{4,5},{5,6},{6,7},{7,8},{8,9},{9,10},{10,1... | collective-permute-start | bytes 3145736 | tf_op jit(solution)/shard_map/ppermute | solution.py:57
  56.2 3.4 %copy-start = (bf16[3,4,64,1024]{3,2,1,0:T(8,128)(2,1)}, bf16[3,4,64,1024]{3,2,1,0:T(8,128)(2,1)S(1)}, u32[]{:S(2)}) copy-start(bf16[3,4,64,1024]{3,2,1,0:T(8,128)(2,1)S(1)} %pad_maximum_fusion.refs_2_) | copy-start | bytes 4718596
  56.2 62.7 %copy-start.4 = (s32[1,4,8]{2,1,0:T(4,128)S(1)}, s32[1,4,8]{2,1,0:T(4,128)}, u32[]{:S(2)}) copy-start(s32[1,4,8]{2,1,0:T(4,128)} %param.12) | copy-start | bytes 388
  56.2 63.3 %collective-permute-start.9 = (bf16[3,4,64,1024]{3,2,1,0:T(8,128)(2,1)S(1)}, bf16[3,4,64,1024]{3,2,1,0:T(8,128)(2,1)}, u32[]{:S(2)}, u32[]{:S(2)}) collective-permute-start(bf16[3,4,64,1024]{3,2,1,0:T(8,128)(2,1)S(1)} %pad_maximum_fusion.refs_2_), channel_id=1, source_target_pairs={{0,64},{1,65},{2,66},{3,67},{4,68},{5,69},{6,70},{7,71},{8,72},{9,... | collective-permute-start | bytes 4718600 | tf_op jit(solution)/shard_map/ppermute | solution.py:57
  59.6 31.0 %collective-permute-start.8 = (bf16[3,2,64,1024]{3,2,1,0:T(8,128)(2,1)S(1)}, bf16[3,2,64,1024]{3,2,1,0:T(8,128)(2,1)}, u32[]{:S(2)}, u32[]{:S(2)}) collective-permute-start(bf16[3,2,64,1024]{3,2,1,0:T(8,128)(2,1)S(1)} %get-tuple-element.14), channel_id=1, source_target_pairs={{0,48},{1,49},{2,50},{3,51},{4,52},{5,53},{6,54},{7,55},{8,56},{9,... | collective-permute-start | bytes 2359304 | tf_op jit(solution)/shard_map/ppermute | solution.py:57
  61.5 54.7 %collective-permute-start.11 = (bf16[3,2,64,1024]{3,2,1,0:T(8,128)(2,1)S(1)}, bf16[3,2,64,1024]{3,2,1,0:T(8,128)(2,1)S(1)}, u32[]{:S(2)}, u32[]{:S(2)}) collective-permute-start(bf16[3,2,64,1024]{3,2,1,0:T(8,128)(2,1)S(1)} %get-tuple-element.13), channel_id=1, source_target_pairs={{0,16},{1,17},{2,18},{3,19},{4,20},{5,21},{6,22},{7,23},{8,24},{9,... | collective-permute-start | bytes 2359304 | tf_op jit(solution)/shard_map/ppermute | solution.py:57
  78.6 63.0 %collective-permute-start.3 = (bf16[512,1024]{1,0:T(8,128)(2,1)}, bf16[512,1024]{1,0:T(8,128)(2,1)S(1)}, u32[]{:S(2)}, u32[]{:S(2)}) collective-permute-start(bf16[512,1024]{1,0:T(8,128)(2,1)} %collective-permute-done.2.high), channel_id=1, source_target_pairs={{1,0},{2,1},{3,2},{4,3},{5,4},{6,5},{7,6},{8,7},{9,8},{10,9},{11,1... | collective-permute-start | bytes 3145736 | tf_op jit(solution)/shard_map/ppermute | solution.py:57
  88.7 52.8 %collective-permute-start.1 = (bf16[512,1024]{1,0:T(8,128)(2,1)}, bf16[512,1024]{1,0:T(8,128)(2,1)}, u32[]{:S(2)}, u32[]{:S(2)}) collective-permute-start(bf16[512,1024]{1,0:T(8,128)(2,1)} %collective-permute-done.low), channel_id=1, source_target_pairs={{0,1},{1,2},{2,3},{3,4},{4,5},{5,6},{6,7},{7,8},{8,9},{9,10},{10,1... | collective-permute-start | bytes 3145736 | tf_op jit(solution)/shard_map/ppermute | solution.py:57
  90.6 28.8 %collective-permute-start.10 = (bf16[3,2,64,1024]{3,2,1,0:T(8,128)(2,1)}, bf16[3,2,64,1024]{3,2,1,0:T(8,128)(2,1)}, u32[]{:S(2)}, u32[]{:S(2)}) collective-permute-start(bf16[3,2,64,1024]{3,2,1,0:T(8,128)(2,1)} %collective-permute-done.8.refs_3_), channel_id=1, source_target_pairs={{0,64},{1,65},{2,66},{3,67},{4,68},{5,69},{6,70},{7,71},{8,72},{9,... | collective-permute-start | bytes 2359304 | tf_op jit(solution)/shard_map/ppermute | solution.py:57
  116.2 9.0 %copy-start.3 = (bf16[3,2,64,1024]{3,2,1,0:T(8,128)(2,1)}, bf16[3,2,64,1024]{3,2,1,0:T(8,128)(2,1)S(1)}, u32[]{:S(2)}) copy-start(bf16[3,2,64,1024]{3,2,1,0:T(8,128)(2,1)S(1)} %collective-permute-done.11.refs_3_) | copy-start | bytes 2359300
  116.2 9.0 %collective-permute-start.12 = (bf16[3,2,64,1024]{3,2,1,0:T(8,128)(2,1)S(1)}, bf16[3,2,64,1024]{3,2,1,0:T(8,128)(2,1)}, u32[]{:S(2)}, u32[]{:S(2)}) collective-permute-start(bf16[3,2,64,1024]{3,2,1,0:T(8,128)(2,1)S(1)} %collective-permute-done.11.refs_3_), channel_id=1, source_target_pairs={{0,64},{1,65},{2,66},{3,67},{4,68},{5,69},{6,70},{7,71},{8,72},{9,... | collective-permute-start | bytes 2359304 | tf_op jit(solution)/shard_map/ppermute | solution.py:57
  141.5 1.0 copy-start.2
